TPU v7x, 32 devices: a whole 2x2x4 slice. The times are simulated.
32 devices in a mesh: dp: 4 (over y, x), ctx: 8 (over z, core).
Axes of the slice: x: 2, y: 2, z: 4, core: 2. Of those that a mesh axis runs over, the one named last changes fastest.
Arguments:
- inputs: bfloat16 [8, 2048, 768], P('dp', 'ctx'), may hold values from -6 to 6
- segments: int32 [8, 2048], P('dp', 'ctx'), may hold values from 0 to 7, never falling along the last dimension, each value on 1 to 1024 neighbouring positions
- w_qkv: bfloat16 [768, 2304], P(('dp', 'ctx')), may hold values from -0.21875 to 0.21875
- b_query: bfloat16 [768], P(('dp', 'ctx')), may hold values from -3 to 3
- b_value: bfloat16 [768], P(('dp', 'ctx')), may hold values from -1.75 to 1.75
- w_out: bfloat16 [768, 768], P(('dp', 'ctx')), may hold values from -2.5 to 2.5
- b_attn: bfloat16 [768], P(('dp', 'ctx')), may hold values from -1.75 to 1.75
- gain_one: bfloat16 [768], P(('dp', 'ctx')), may hold values from 0.5 to 1.5
- shift_one: bfloat16 [768], P(('dp', 'ctx')), may hold values from -1.75 to 1.75
- w_in: bfloat16 [768, 3072], P(('dp', 'ctx')), may hold values from -0.21875 to 0.21875
- b_in: bfloat16 [3072], P(('dp', 'ctx')), may hold values from -1.75 to 1.75
- w_back: bfloat16 [3072, 768], P(('dp', 'ctx')), may hold values from -0.109375 to 0.109375
- b_back: bfloat16 [768], P(('dp', 'ctx')), may hold values from -1.75 to 1.75
- gain_two: bfloat16 [768], P(('dp', 'ctx')), may hold values from 0.5 to 1.5
- shift_two: bfloat16 [768], P(('dp', 'ctx')), may hold values from -1.75 to 1.75
- cotangent: bfloat16 [8, 2048, 768], P('dp', 'ctx'), may hold values from -6 to 6
Outputs:
- output: bfloat16 [8, 2048, 768], P('dp', 'ctx')
- input_grad: float32 [8, 2048, 768], P('dp', 'ctx')
- grad_w_qkv: float32 [768, 2304], P(('dp', 'ctx'))
- grad_b_query: float32 [768], P(('dp', 'ctx'))
- grad_b_value: float32 [768], P(('dp', 'ctx'))
- grad_w_out: float32 [768, 768], P(('dp', 'ctx'))
- grad_b_attn: float32 [768], P(('dp', 'ctx'))
- grad_gain_one: float32 [768], P(('dp', 'ctx'))
- grad_shift_one: float32 [768], P(('dp', 'ctx'))
- grad_w_in: float32 [768, 3072], P(('dp', 'ctx'))
- grad_b_in: float32 [3072], P(('dp', 'ctx'))
- grad_w_back: float32 [3072, 768], P(('dp', 'ctx'))
- grad_b_back: float32 [768], P(('dp', 'ctx'))
- grad_gain_two: float32 [768], P(('dp', 'ctx'))
- grad_shift_two: float32 [768], P(('dp', 'ctx'))
Inputs may be any that keep to these rules, and one draw needn't show every extreme that they name: `segments`: within each sequence segment numbers never fall; every document has 1 to 1024 tokens, and one of them has exactly that many.
All inputs are finite; a program needn't handle non-finite values.
Results may differ from a plain program's by a relative error of at most 0.015.
Values may be sent and summed in bfloat16 or wider, within the bound.
A program may use at most 192 MiB of HBM per device.

v0:
```python
import jax
import jax.numpy as jnp
from jax import lax
from jax.sharding import PartitionSpec as P

HEADS = 12
HEAD_DIM = 64


negative_fill = -1e30
layer_eps = 1e-12


def layer_norm(resid, gain, shift):
    center = resid - jnp.mean(resid, axis=-1, keepdims=True)
    spread = jnp.mean(center * center, axis=-1, keepdims=True)
    return center * lax.rsqrt(spread + layer_eps) * gain + shift


def gelu_exact(values):
    return jax.nn.gelu(values, approximate=False)


def attend_forward(entries):
    query_rows, key_rows, value_rows, query_ids, key_ids = entries
    scores = jnp.einsum(
        "qhd,khd->hqk", query_rows, key_rows, preferred_element_type=jnp.float32
    ) * HEAD_DIM ** (-0.5)
    allowed = (query_ids[:, None] == key_ids[None, :])[None]
    scores = jnp.where(allowed, scores, negative_fill)
    peak = jnp.max(scores, axis=-1, keepdims=True)
    raised = jnp.exp(scores - peak)
    total = jnp.sum(raised, axis=-1, keepdims=True)
    probs_low = (raised / total).astype(jnp.bfloat16)
    context = jnp.einsum("hqk,khd->qhd", probs_low, value_rows, preferred_element_type=jnp.float32)
    return (context, (peak + jnp.log(total))[..., 0])


def score_terms(query_rows, key_rows, value_rows, grad_context, log_total, query_ids, key_ids):
    scale = HEAD_DIM ** (-0.5)
    scores = (
        jnp.einsum("qhd,khd->hqk", query_rows, key_rows, preferred_element_type=jnp.float32) * scale
    )
    allowed = (query_ids[:, None] == key_ids[None, :])[None]
    probs = jnp.where(allowed, jnp.exp(scores - log_total[..., None]), 0.0)
    d_probs = jnp.einsum(
        "qhd,khd->hqk", grad_context, value_rows, preferred_element_type=jnp.float32
    )
    return (probs, d_probs)


def attend_backward(entries):
    query_rows, key_rows, value_rows, grad_context, log_total, query_ids, key_ids = entries
    scale = HEAD_DIM ** (-0.5)
    probs, d_probs = score_terms(
        query_rows, key_rows, value_rows, grad_context, log_total, query_ids, key_ids
    )
    inner = jnp.sum(probs * d_probs, axis=-1, keepdims=True)
    d_scores = (probs * (d_probs - inner)).astype(jnp.bfloat16)
    d_queries = (
        jnp.einsum("hqk,khd->qhd", d_scores, key_rows, preferred_element_type=jnp.float32) * scale
    )
    d_keys = (
        jnp.einsum("hqk,qhd->khd", d_scores, query_rows, preferred_element_type=jnp.float32) * scale
    )
    d_values = jnp.einsum(
        "hqk,qhd->khd", probs.astype(jnp.bfloat16), grad_context, preferred_element_type=jnp.float32
    )
    length = key_rows.shape[0]
    return (
        d_queries,
        d_keys.reshape(length, HEADS * HEAD_DIM),
        d_values.reshape(length, HEADS * HEAD_DIM),
    )


def on_device(
    inputs,
    segments,
    w_qkv,
    b_query,
    b_value,
    w_out,
    b_attn,
    gain_one,
    shift_one,
    w_in,
    b_in,
    w_back,
    b_back,
    gain_two,
    shift_two,
    cotangent,
):
    seq_count, group_len, model_width = inputs.shape
    tok_count = seq_count * group_len
    gathered = (
        lax.all_gather(w_qkv, ("dp", "ctx"), axis=0, tiled=True),
        lax.all_gather(b_query, ("dp", "ctx"), axis=0, tiled=True),
        lax.all_gather(b_value, ("dp", "ctx"), axis=0, tiled=True),
        lax.all_gather(w_out, ("dp", "ctx"), axis=0, tiled=True),
        lax.all_gather(b_attn, ("dp", "ctx"), axis=0, tiled=True),
        lax.all_gather(gain_one, ("dp", "ctx"), axis=0, tiled=True),
        lax.all_gather(shift_one, ("dp", "ctx"), axis=0, tiled=True),
        lax.all_gather(w_in, ("dp", "ctx"), axis=0, tiled=True),
        lax.all_gather(b_in, ("dp", "ctx"), axis=0, tiled=True),
        lax.all_gather(w_back, ("dp", "ctx"), axis=0, tiled=True),
        lax.all_gather(b_back, ("dp", "ctx"), axis=0, tiled=True),
        lax.all_gather(gain_two, ("dp", "ctx"), axis=0, tiled=True),
        lax.all_gather(shift_two, ("dp", "ctx"), axis=0, tiled=True),
    )
    (
        wide_qkv,
        full_b_query,
        full_b_value,
        wide_out,
        full_b_attn,
        full_gain_one,
        full_shift_one,
        wide_in,
        full_b_in,
        wide_back,
        full_b_back,
        full_gain_two,
        full_shift_two,
    ) = gathered
    tokens = inputs.reshape(tok_count, model_width)
    projected = jnp.dot(tokens, wide_qkv, preferred_element_type=jnp.float32)
    query_low = (projected[:, :model_width] + full_b_query.astype(jnp.float32)).astype(jnp.bfloat16)
    key_low = projected[:, model_width : 2 * model_width].astype(jnp.bfloat16)
    value_low = (projected[:, 2 * model_width :] + full_b_value.astype(jnp.float32)).astype(
        jnp.bfloat16
    )
    key_ids = lax.all_gather(segments, "ctx", axis=1, tiled=True)
    key_local = key_low.reshape(seq_count, group_len, model_width)
    value_local = value_low.reshape(seq_count, group_len, model_width)
    key_whole, value_whole = (
        lax.all_gather(key_local, "ctx", axis=1, tiled=True),
        lax.all_gather(value_local, "ctx", axis=1, tiled=True),
    )
    seq_len = key_whole.shape[1]
    query_heads = query_low.reshape(seq_count, group_len, HEADS, HEAD_DIM)
    context, log_total = lax.map(
        attend_forward,
        (
            query_heads,
            key_whole.reshape(seq_count, seq_len, HEADS, HEAD_DIM),
            value_whole.reshape(seq_count, seq_len, HEADS, HEAD_DIM),
            segments,
            key_ids,
        ),
    )
    attended = context.reshape(tok_count, model_width).astype(jnp.bfloat16)
    attn_out = jnp.dot(attended, wide_out, preferred_element_type=jnp.float32) + full_b_attn.astype(
        jnp.float32
    )
    resid_one = tokens.astype(jnp.float32) + attn_out
    normed, norm_one_back = jax.vjp(
        layer_norm, resid_one, full_gain_one.astype(jnp.float32), full_shift_one.astype(jnp.float32)
    )
    normed_low = normed.astype(jnp.bfloat16)
    pre_act = jnp.dot(normed_low, wide_in, preferred_element_type=jnp.float32) + full_b_in.astype(
        jnp.float32
    )
    activ_f, gelu_back = jax.vjp(gelu_exact, pre_act)
    activ = activ_f.astype(jnp.bfloat16)
    branch = jnp.dot(activ, wide_back, preferred_element_type=jnp.float32) + full_b_back.astype(
        jnp.float32
    )
    resid_two = normed + branch
    final_norm, norm_two_back = jax.vjp(
        layer_norm, resid_two, full_gain_two.astype(jnp.float32), full_shift_two.astype(jnp.float32)
    )
    output = final_norm.astype(jnp.bfloat16).reshape(seq_count, group_len, model_width)
    back_qkv, back_out, back_in, back_back = (
        lax.all_gather(w_qkv, ("dp", "ctx"), axis=0, tiled=True),
        lax.all_gather(w_out, ("dp", "ctx"), axis=0, tiled=True),
        lax.all_gather(w_in, ("dp", "ctx"), axis=0, tiled=True),
        lax.all_gather(w_back, ("dp", "ctx"), axis=0, tiled=True),
    )
    d_final = cotangent.reshape(tok_count, model_width).astype(jnp.float32)
    d_two, grad_gain_two, grad_shift_two = norm_two_back(d_final)
    d_branch = d_two.astype(jnp.bfloat16)
    grad_b_back = jnp.sum(d_branch.astype(jnp.float32), axis=0)
    grad_w_back = jnp.einsum("tf,td->fd", activ, d_branch, preferred_element_type=jnp.float32)
    d_activ = jnp.einsum("td,fd->tf", d_branch, back_back, preferred_element_type=jnp.float32)
    d_pre = gelu_back(d_activ)[0].astype(jnp.bfloat16)
    grad_b_in = jnp.sum(d_pre.astype(jnp.float32), axis=0)
    grad_w_in = jnp.einsum("td,tf->df", normed_low, d_pre, preferred_element_type=jnp.float32)
    d_normed = d_two + jnp.einsum("tf,df->td", d_pre, back_in, preferred_element_type=jnp.float32)
    d_one, grad_gain_one, grad_shift_one = norm_one_back(d_normed)
    d_attn = d_one.astype(jnp.bfloat16)
    grad_b_attn = jnp.sum(d_attn.astype(jnp.float32), axis=0)
    grad_w_out = jnp.einsum("ti,td->id", attended, d_attn, preferred_element_type=jnp.float32)
    d_attended = jnp.einsum(
        "td,id->ti", d_attn, back_out, preferred_element_type=jnp.float32
    ).astype(jnp.bfloat16)
    key_back, value_back = (
        lax.all_gather(key_local, "ctx", axis=1, tiled=True),
        lax.all_gather(value_local, "ctx", axis=1, tiled=True),
    )
    grad_heads = d_attended.reshape(seq_count, group_len, HEADS, HEAD_DIM)
    d_query_part, d_key_part, d_value_part = lax.map(
        attend_backward,
        (
            query_heads,
            key_back.reshape(seq_count, seq_len, HEADS, HEAD_DIM),
            value_back.reshape(seq_count, seq_len, HEADS, HEAD_DIM),
            grad_heads,
            log_total,
            segments,
            key_ids,
        ),
    )
    d_key_sum, d_value_sum = (
        lax.psum_scatter(
            d_key_part.astype(jnp.bfloat16), "ctx", scatter_dimension=1, tiled=True
        ).astype(jnp.float32),
        lax.psum_scatter(
            d_value_part.astype(jnp.bfloat16), "ctx", scatter_dimension=1, tiled=True
        ).astype(jnp.float32),
    )
    d_queries = d_query_part.reshape(tok_count, model_width).astype(jnp.bfloat16)
    d_keys = d_key_sum.reshape(tok_count, model_width).astype(jnp.bfloat16)
    d_values = d_value_sum.reshape(tok_count, model_width).astype(jnp.bfloat16)
    d_proj = jnp.concatenate([d_queries, d_keys, d_values], axis=1)
    grad_w_qkv = jnp.einsum("td,te->de", tokens, d_proj, preferred_element_type=jnp.float32)
    grad_b_query = jnp.sum(d_queries.astype(jnp.float32), axis=0)
    grad_b_value = jnp.sum(d_values.astype(jnp.float32), axis=0)
    input_grad = d_one + jnp.einsum(
        "te,de->td", d_proj, back_qkv, preferred_element_type=jnp.float32
    )
    summed = (
        lax.psum_scatter(grad_w_qkv, ("dp", "ctx"), scatter_dimension=0, tiled=True),
        lax.psum_scatter(grad_b_query, ("dp", "ctx"), scatter_dimension=0, tiled=True),
        lax.psum_scatter(grad_b_value, ("dp", "ctx"), scatter_dimension=0, tiled=True),
        lax.psum_scatter(grad_w_out, ("dp", "ctx"), scatter_dimension=0, tiled=True),
        lax.psum_scatter(grad_b_attn, ("dp", "ctx"), scatter_dimension=0, tiled=True),
        lax.psum_scatter(grad_gain_one, ("dp", "ctx"), scatter_dimension=0, tiled=True),
        lax.psum_scatter(grad_shift_one, ("dp", "ctx"), scatter_dimension=0, tiled=True),
        lax.psum_scatter(grad_w_in, ("dp", "ctx"), scatter_dimension=0, tiled=True),
        lax.psum_scatter(grad_b_in, ("dp", "ctx"), scatter_dimension=0, tiled=True),
        lax.psum_scatter(grad_w_back, ("dp", "ctx"), scatter_dimension=0, tiled=True),
        lax.psum_scatter(grad_b_back, ("dp", "ctx"), scatter_dimension=0, tiled=True),
        lax.psum_scatter(grad_gain_two, ("dp", "ctx"), scatter_dimension=0, tiled=True),
        lax.psum_scatter(grad_shift_two, ("dp", "ctx"), scatter_dimension=0, tiled=True),
    )
    return (
        output,
        input_grad.reshape(seq_count, group_len, model_width),
        summed[0],
        summed[1],
        summed[2],
        summed[3],
        summed[4],
        summed[5],
        summed[6],
        summed[7],
        summed[8],
        summed[9],
        summed[10],
        summed[11],
        summed[12],
    )


def solution(mesh):
    placed = (
        P("dp", "ctx", None),
        P("dp", "ctx"),
        P(("dp", "ctx"), None),
        P(("dp", "ctx")),
        P(("dp", "ctx")),
        P(("dp", "ctx"), None),
        P(("dp", "ctx")),
        P(("dp", "ctx")),
        P(("dp", "ctx")),
        P(("dp", "ctx"), None),
        P(("dp", "ctx")),
        P(("dp", "ctx"), None),
        P(("dp", "ctx")),
        P(("dp", "ctx")),
        P(("dp", "ctx")),
        P("dp", "ctx", None),
    )
    return jax.shard_map(
        on_device,
        mesh=mesh,
        in_specs=placed,
        out_specs=(
            P("dp", "ctx", None),
            P("dp", "ctx", None),
            P(("dp", "ctx"), None),
            P(("dp", "ctx")),
            P(("dp", "ctx")),
            P(("dp", "ctx"), None),
            P(("dp", "ctx")),
            P(("dp", "ctx")),
            P(("dp", "ctx")),
            P(("dp", "ctx"), None),
            P(("dp", "ctx")),
            P(("dp", "ctx"), None),
            P(("dp", "ctx")),
            P(("dp", "ctx")),
            P(("dp", "ctx")),
        ),
        check_vma=False,
    )
```

profile of v0, /device:TPU:28, one launch (start us, length us, event | category | flops | bytes accessed | tf_op | source)
XLA Modules:
  0.0 1262.5 jit_solution(12611655410761532791)
XLA Ops:
  15.5 40.4 %all-reduce.19 = (bf16[768]{0:T(1024)(128)(2,1)S(1)}, bf16[768]{0:T(1024)(128)(2,1)S(1)}, bf16[768]{0:T(1024)(128)(2,1)S(1)}, bf16[768]{0:T(1024)(128)(2,1)S(1)}...) all-reduce(bf16[768]{0:T(1024)(128)(2,1)S(1)} %dynamic-update-slice, ...), channel_id=1, replica_groups=mesh['dp'=4,'ctx'=8] {'dp','ctx'}, use_global_device_ids=true, to_apply=%add | all-reduce | flops 9216 | bytes 36864
  56.0 14.8 %all-gather.7.cloned.1.call-done = bf16[768,2304]{1,0:T(8,128)(2,1)} async-done(((bf16[24,2304]{1,0:T(8,128)(2,1)}), bf16[768,2304]{1,0:T(8,128)(2,1)}) %all-gather.7.cloned.1.call-update) | async-done | bytes 3538960 | tf_op jit(solution)/shard_map/all_gather | solution.py:98
  70.8 4.3 fusion.83
  75.0 2.1 copy-done.11
  77.2 1.2 fusion.63
  78.4 2.4 slice.23
  82.6 11.9 all_gather.57
  100.2 40.7 %all-gather.9.cloned.1.call-done = bf16[2,2048,768]{2,1,0:T(8,128)(2,1)} async-done(((bf16[2,256,768]{2,1,0:T(8,128)(2,1)}), bf16[2,2048,768]{2,1,0:T(8,128)(2,1)}) %all-gather.9.cloned.1.call-update) | async-done | bytes 6291472 | tf_op jit(solution)/shard_map/all_gather | solution.py:139
  140.9 8.7 copy.51
  149.5 56.9 %all-gather.11.cloned.1.call-done = bf16[2,2048,768]{2,1,0:T(8,128)(2,1)} async-done(((bf16[2,256,768]{2,1,0:T(8,128)(2,1)}), bf16[2,2048,768]{2,1,0:T(8,128)(2,1)}) %all-gather.11.cloned.1.call-update) | async-done | bytes 6291472 | tf_op jit(solution)/shard_map/all_gather | solution.py:138
  206.4 8.7 copy.53
  215.3 79.2 %while.26 = (s32[]{:T(128)}, bf16[2,256,12,64]{1,3,2,0:T(8,128)(2,1)S(1)}, f32[2,12,256]{2,1,0:T(8,128)S(1)}, bf16[2,2048,12,64]{1,3,2,0:T(8,128)(2,1)}, s32[2,2...) while((s32[]{:T(128)}, ...), condition=%wide.region_3.4_spmd, body=%wide.region_0.3_spmd.sunk | while | flops 1686631424 | bytes 85214304 | solution.py:143
  215.7 14.6 %fusion.124 = (f32[12,256]{1,0:T(8,128)S(1)}, f32[12,256,2048]{2,1,0:T(8,128)}) fusion(pred[256,2048]{1,0:T(8,128)(4,1)S(1)} %broadcast_compare_fusion.4, bf16[2,2048,12,64]{1,3,2,0:T(8,128)(2,1)} %get-tuple-element.465, s32[]{:T(128)} %get-tuple-element.449, bf16[2,256,12,64]{1,3,2,0:T(8,128)(2,1)} %get-tuple-element.464), kind=kOutput, calls=%fused_computation.3.clone.1 | convolution fusion | flops 824177664 | bytes 29242368 | tf_op jit(solution)/shard_map/while/body/eval_jaxpr/qhd,khd->hqk/dot_general | solution.py:26
  230.3 11.6 fusion.125
  241.9 12.7 %fusion.126 = bf16[2,256,12,64]{1,3,2,0:T(8,128)(2,1)S(1)} fusion(bf16[2,256,12,64]{1,3,2,0:T(8,128)(2,1)S(1)} %get-tuple-element.450, s32[]{:T(128)} %get-tuple-element.449, f32[12,256,2048]{2,1,0:T(8,128)} %get-tuple-element.423, f32[12,256]{1,0:T(8,128)S(1)} %fusion.125, f32[12,256]{1,0:T(8,128)S(1)} %get-tuple-element.424, ...), kind=kOutput, calls=%fused_computation.12.clone.1 | convolution fusion | flops 836763648 | bytes 29656064 | tf_op jit(solution)/shard_map/while/body/eval_jaxpr/hqk,khd->qhd/dot_general | solution.py:35
  255.0 14.7 %fusion.124 = (f32[12,256]{1,0:T(8,128)S(1)}, f32[12,256,2048]{2,1,0:T(8,128)}) fusion(pred[256,2048]{1,0:T(8,128)(4,1)S(1)} %broadcast_compare_fusion.4, bf16[2,2048,12,64]{1,3,2,0:T(8,128)(2,1)} %get-tuple-element.465, s32[]{:T(128)} %get-tuple-element.449, bf16[2,256,12,64]{1,3,2,0:T(8,128)(2,1)} %get-tuple-element.464), kind=kOutput, calls=%fused_computation.3.clone.1 | convolution fusion | flops 824177664 | bytes 29242368 | tf_op jit(solution)/shard_map/while/body/eval_jaxpr/qhd,khd->hqk/dot_general | solution.py:26
  269.7 11.6 fusion.125
  281.4 12.7 %fusion.126 = bf16[2,256,12,64]{1,3,2,0:T(8,128)(2,1)S(1)} fusion(bf16[2,256,12,64]{1,3,2,0:T(8,128)(2,1)S(1)} %get-tuple-element.450, s32[]{:T(128)} %get-tuple-element.449, f32[12,256,2048]{2,1,0:T(8,128)} %get-tuple-element.423, f32[12,256]{1,0:T(8,128)S(1)} %fusion.125, f32[12,256]{1,0:T(8,128)S(1)} %get-tuple-element.424, ...), kind=kOutput, calls=%fused_computation.12.clone.1 | convolution fusion | flops 836763648 | bytes 29656064 | tf_op jit(solution)/shard_map/while/body/eval_jaxpr/hqk,khd->qhd/dot_general | solution.py:35
  295.6 2.7 fusion.81
  298.6 29.6 %all-gather.15.cloned.1.call-done = bf16[768,3072]{1,0:T(8,128)(2,1)} async-done(((bf16[24,3072]{1,0:T(8,128)(2,1)}), bf16[768,3072]{1,0:T(8,128)(2,1)}) %all-gather.15.cloned.1.call-update) | async-done | bytes 4718608 | tf_op jit(solution)/shard_map/all_gather | solution.py:105
  328.2 19.8 %multiply_convert_fusion.1 = (bf16[512,3072]{1,0:T(8,128)(2,1)}, f32[512,3072]{1,0:T(8,128)}, f32[512,3072]{1,0:T(8,128)}) fusion(f32[3072]{0:T(1024)S(1)} %copy-done.31, bf16[768,3072]{1,0:T(8,128)(2,1)} %all-gather.15.cloned.1.call-done, f32[512,768]{1,0:T(8,128)S(1)} %get-tuple-element.307, f32[768]{0:T(1024)S(1)} %copy-done.37, f32[768]{0:T(1024)S(1)} %copy-done.29, ...), kind=kOutput, calls=%fused_computation.67 | convolution fusion | flops 2521694208 | bytes 22042624 | tf_op jit(solution)/shard_map/dot_general | solution.py:162
  348.0 45.1 %all-gather.17.cloned.1.call-done = bf16[3072,768]{1,0:T(8,128)(2,1)} async-done(((bf16[96,768]{1,0:T(8,128)(2,1)}), bf16[3072,768]{1,0:T(8,128)(2,1)}) %all-gather.17.cloned.1.call-update) | async-done | bytes 4718608 | tf_op jit(solution)/shard_map/all_gather | solution.py:107
  393.1 6.2 fusion.82
  399.6 1.3 fusion.68
  400.9 1.6 fusion.79
  403.3 9.0 convert_reduce_fusion
  412.3 3.7 multiply_reduce_fusion.1
  416.7 1.1 copy-done.9
  422.8 181.2 %while.27 = (s32[]{:T(128)}, bf16[2,256,12,64]{1,3,2,0:T(8,128)(2,1)}, bf16[2,2048,768]{2,1,0:T(8,128)(2,1)}, bf16[2,2048,768]{2,1,0:T(8,128)(2,1)}, bf16[2,2048...) while((s32[]{:T(128)}, ...), condition=%wide.region_14.15_spmd, body=%wide.region_12.14_spmd.sunk | while | flops 4124767232 | bytes 311807776 | solution.py:203
  423.3 14.0 %fusion.135 = f32[12,256,2048]{2,1,0:T(8,128)} fusion(bf16[2,2048,12,64]{1,3,2,0:T(8,128)(2,1)} %get-tuple-element.495, s32[]{:T(128)} %get-tuple-element.479, bf16[2,256,12,64]{1,3,2,0:T(8,128)(2,1)} %get-tuple-element.498), kind=kOutput, calls=%fused_computation.34.clone.1 | convolution fusion | flops 805306368 | bytes 28705792 | tf_op jit(solution)/shard_map/while/body/eval_jaxpr/qhd,khd->hqk/dot_general | solution.py:42
  437.3 19.1 %multiply_reduce_fusion.6 = (f32[12,256]{1,0:T(8,128)S(1)}, f32[12,256,2048]{2,1,0:T(8,128)}) fusion(f32[12,256,2048]{2,1,0:T(8,128)} %fusion.135, f32[12,256]{1,0:T(8,128)S(1)} %dynamic-slice_bitcast_fusion.2, pred[256,2048]{1,0:T(8,128)(4,1)S(1)} %broadcast_compare_fusion.5, bf16[2,2048,12,64]{1,3,2,0:T(8,128)(2,1)} %get-tuple-element.501, ...), kind=kOutput, calls=%fused_computation.24.clone.1 | convolution fusion | flops 836760576 | bytes 54420480 | tf_op jit(solution)/shard_map/while/body/eval_jaxpr/qhd,khd->hqk/dot_general | solution.py:46
  456.4 16.9 %multiply_convert_fusion.3 = bf16[12,256,2048]{2,1,0:T(8,128)(2,1)S(1)} fusion(f32[12,256,2048]{2,1,0:T(8,128)} %get-tuple-element.436, f32[12,256,2048]{2,1,0:T(8,128)} %fusion.135, f32[12,256]{1,0:T(8,128)S(1)} %get-tuple-element.437, f32[12,256]{1,0:T(8,128)S(1)} %dynamic-slice_bitcast_fusion.2, pred[256,2048]{1,0:T(8,128)(4,1)S(1)} %broadcast_compare_fusion.5), kind=kLoop, calls=%fused_computation.23.clone.1 | loop fusion | flops 37748736 | bytes 63463424 | tf_op jit(solution)/shard_map/while/body/eval_jaxpr/convert_element_type | solution.py:59
  473.2 3.6 convolution_multiply_fusion.2
  477.8 2.8 copy.93
  480.6 12.5 fusion.137
  493.1 4.8 copy.92
  497.9 6.0 constant_dynamic-update-slice_fusion.3
  504.0 8.5 fusion.136
  513.8 14.0 %fusion.135 = f32[12,256,2048]{2,1,0:T(8,128)} fusion(bf16[2,2048,12,64]{1,3,2,0:T(8,128)(2,1)} %get-tuple-element.495, s32[]{:T(128)} %get-tuple-element.479, bf16[2,256,12,64]{1,3,2,0:T(8,128)(2,1)} %get-tuple-element.498), kind=kOutput, calls=%fused_computation.34.clone.1 | convolution fusion | flops 805306368 | bytes 28705792 | tf_op jit(solution)/shard_map/while/body/eval_jaxpr/qhd,khd->hqk/dot_general | solution.py:42
  527.7 19.1 %multiply_reduce_fusion.6 = (f32[12,256]{1,0:T(8,128)S(1)}, f32[12,256,2048]{2,1,0:T(8,128)}) fusion(f32[12,256,2048]{2,1,0:T(8,128)} %fusion.135, f32[12,256]{1,0:T(8,128)S(1)} %dynamic-slice_bitcast_fusion.2, pred[256,2048]{1,0:T(8,128)(4,1)S(1)} %broadcast_compare_fusion.5, bf16[2,2048,12,64]{1,3,2,0:T(8,128)(2,1)} %get-tuple-element.501, ...), kind=kOutput, calls=%fused_computation.24.clone.1 | convolution fusion | flops 836760576 | bytes 54420480 | tf_op jit(solution)/shard_map/while/body/eval_jaxpr/qhd,khd->hqk/dot_general | solution.py:46
  546.8 16.9 %multiply_convert_fusion.3 = bf16[12,256,2048]{2,1,0:T(8,128)(2,1)S(1)} fusion(f32[12,256,2048]{2,1,0:T(8,128)} %get-tuple-element.436, f32[12,256,2048]{2,1,0:T(8,128)} %fusion.135, f32[12,256]{1,0:T(8,128)S(1)} %get-tuple-element.437, f32[12,256]{1,0:T(8,128)S(1)} %dynamic-slice_bitcast_fusion.2, pred[256,2048]{1,0:T(8,128)(4,1)S(1)} %broadcast_compare_fusion.5), kind=kLoop, calls=%fused_computation.23.clone.1 | loop fusion | flops 37748736 | bytes 63463424 | tf_op jit(solution)/shard_map/while/body/eval_jaxpr/convert_element_type | solution.py:59
  563.7 3.6 convolution_multiply_fusion.2
  568.3 2.8 copy.93
  571.1 12.5 fusion.137
  583.5 4.8 copy.92
  588.4 6.0 constant_dynamic-update-slice_fusion.3
  594.4 8.5 fusion.136
  605.3 2.2 fusion.84
  607.6 7.2 fusion.74
  615.0 1.1 copy-done.20
  616.0 8.2 fusion.85
  626.4 45.1 %reduce-scatter.9.cloned.1.call-done = bf16[2,256,768]{2,1,0:T(8,128)(2,1)} async-done(((bf16[2,2048,768]{2,1,0:T(8,128)(2,1)}), bf16[2,256,768]{2,1,0:T(8,128)(2,1)}) %reduce-scatter.9.cloned.1.call-update) | async-done | bytes 786448 | tf_op jit(solution)/shard_map/reduce_scatter | solution.py:216
  671.4 1.4 copy.62
  672.9 69.1 %reduce-scatter.11.cloned.1.call-done = bf16[2,256,768]{2,1,0:T(8,128)(2,1)} async-done(((bf16[2,2048,768]{2,1,0:T(8,128)(2,1)}), bf16[2,256,768]{2,1,0:T(8,128)(2,1)}) %reduce-scatter.11.cloned.1.call-update) | async-done | bytes 786448 | tf_op jit(solution)/shard_map/reduce_scatter | solution.py:219
  742.0 1.4 copy.63
  743.4 6.2 convolution_bitcast_fusion
  749.7 8.1 copy.65
  759.3 1.3 convert_reduce_fusion.4
  760.6 41.3 %all-reduce.18 = (f32[768]{0:T(1024)S(1)}, f32[768]{0:T(1024)S(1)}, f32[768]{0:T(1024)S(1)}, f32[768]{0:T(1024)S(1)}, f32[768]{0:T(1024)S(1)}, /*index=5*/f32[30...) all-reduce(f32[768]{0:T(1024)S(1)} %reduce_sum.186, ...), channel_id=5, replica_groups=mesh['dp'=4,'ctx'=8] {'dp','ctx'}, use_global_device_ids=true, to_apply=%region_19.20.clone | all-reduce | flops 9216 | bytes 73728
  807.2 6.0 add_add_fusion.4
  813.2 34.5 %reduce-scatter.13.cloned.1.call-done = f32[24,768]{1,0:T(8,128)} async-done(((f32[768,768]{1,0:T(8,128)}), f32[24,768]{1,0:T(8,128)}) %reduce-scatter.13.cloned.1.call-update) | async-done | bytes 73744 | tf_op jit(solution)/shard_map/reduce_scatter | solution.py:237
  847.7 141.5 %reduce-scatter.15.cloned.1.call-done = f32[24,3072]{1,0:T(8,128)} async-done(((f32[768,3072]{1,0:T(8,128)}), f32[24,3072]{1,0:T(8,128)}) %reduce-scatter.15.cloned.1.call-update) | async-done | bytes 294928 | tf_op jit(solution)/shard_map/reduce_scatter | solution.py:241
  989.2 141.6 %reduce-scatter.17.cloned.1.call-done = f32[96,768]{1,0:T(8,128)} async-done(((f32[3072,768]{1,0:T(8,128)}), f32[96,768]{1,0:T(8,128)}) %reduce-scatter.17.cloned.1.call-update) | async-done | bytes 294928 | tf_op jit(solution)/shard_map/reduce_scatter | solution.py:243
  1130.8 124.6 %reduce-scatter.19.cloned.1.call-done = f32[24,2304]{1,0:T(8,128)} async-done(((f32[768,2304]{1,0:T(8,128)}), f32[24,2304]{1,0:T(8,128)}) %reduce-scatter.19.cloned.1.call-update) | async-done | bytes 221200
  (224 shorter events, 39.6 us)
Async XLA Ops:
  7.2 63.6 %all-gather.7.cloned.1.call-start = ((), (), s32[]{:S(2)}) async-start(), calls=%async_computation.6 | async-start | bytes 3649536 | tf_op jit(solution)/shard_map/all_gather | solution.py:98
  7.9 133.0 %all-gather.9.cloned.1.call-start = ((), (), s32[]{:S(2)}) async-start(), calls=%async_computation.7 | async-start | bytes 7077888 | tf_op jit(solution)/shard_map/all_gather | solution.py:139
  75.0 2.1 copy-start.11
  77.2 5.4 copy-start.21
  78.4 128.1 %all-gather.11.cloned.1.call-start = ((), (), s32[]{:S(2)}) async-start(), calls=%async_computation.8 | async-start | bytes 7077888 | tf_op jit(solution)/shard_map/all_gather | solution.py:138
  80.8 214.8 %all-gather.13.cloned.1.call-start = ((), (), s32[]{:S(2)}) async-start(), calls=%async_computation.9 | async-start | bytes 1216512 | tf_op jit(solution)/shard_map/all_gather | solution.py:101
  81.4 246.8 %all-gather.15.cloned.1.call-start = ((), (), s32[]{:S(2)}) async-start(), calls=%async_computation.10 | async-start | bytes 4866048 | tf_op jit(solution)/shard_map/all_gather | solution.py:105
  82.0 311.1 %all-gather.17.cloned.1.call-start = ((), (), s32[]{:S(2)}) async-start(), calls=%async_computation.11 | async-start | bytes 4866048 | tf_op jit(solution)/shard_map/all_gather | solution.py:107
  82.5 588.9 %reduce-scatter.9.cloned.1.call-start = ((), (), s32[]{:S(2)}) async-start(), calls=%async_computation.12 | async-start | bytes 7077888 | tf_op jit(solution)/shard_map/reduce_scatter | solution.py:216
  215.3 80.3 %copy-start.40 = (f32[768]{0:T(1024)S(1)}, f32[768]{0:T(1024)}, u32[]{:S(2)}) copy-start(f32[768]{0:T(1024)} %convert_element_type.130) | copy-start | bytes 9220
  294.5 33.7 %copy-start.29 = (f32[768]{0:T(1024)S(1)}, f32[768]{0:T(1024)}, u32[]{:S(2)}) copy-start(f32[768]{0:T(1024)} %convert_element_type.131) | copy-start | bytes 9220
  294.5 33.7 %copy-start.31 = (f32[3072]{0:T(1024)S(1)}, f32[3072]{0:T(1024)}, u32[]{:S(2)}) copy-start(f32[3072]{0:T(1024)} %convert_element_type.134) | copy-start | bytes 36868
  294.5 33.7 %copy-start.37 = (f32[768]{0:T(1024)S(1)}, f32[768]{0:T(1024)}, u32[]{:S(2)}) copy-start(f32[768]{0:T(1024)} %convert_element_type.132) | copy-start | bytes 9220
  295.5 52.5 %copy-start.12 = (bf16[96,8,2,256]{3,1,2,0:T(8,128)(2,1)}, bf16[96,8,2,256]{3,1,2,0:T(8,128)(2,1)S(1)}, u32[]{:S(2)}) copy-start(bf16[96,8,2,256]{3,1,2,0:T(8,128)(2,1)S(1)} %copy.88) | copy-start | bytes 2359300
  298.2 117.7 %copy-start.7 = (f32[512,768]{1,0:T(8,128)}, f32[512,768]{1,0:T(8,128)S(1)}, u32[]{:S(2)}) copy-start(f32[512,768]{1,0:T(8,128)S(1)} %get-tuple-element.307) | copy-start | bytes 4718596
  298.3 117.7 %copy-start.23 = (f32[512]{0:T(512)}, f32[512]{0:T(512)S(1)}, u32[]{:S(2)}) copy-start(f32[512]{0:T(512)S(1)} %broadcast_multiply_fusion.1) | copy-start | bytes 6148
  298.6 117.4 %copy-start.33 = (f32[512]{0:T(512)}, f32[512]{0:T(512)S(1)}, u32[]{:S(2)}) copy-start(f32[512]{0:T(512)S(1)} %fusion.70) | copy-start | bytes 6148
  298.6 94.5 %copy-start.39 = (f32[768]{0:T(1024)S(1)}, f32[768]{0:T(1024)}, u32[]{:S(2)}) copy-start(f32[768]{0:T(1024)} %convert_element_type.136) | copy-start | bytes 9220
  393.0 10.3 slice-start.4
  393.0 6.5 copy-start.2
  393.0 6.5 copy-start.22
  393.0 7.8 copy-start.25
  393.1 10.2 slice-start.5
  402.5 9.8 slice-start.2
  403.3 9.0 copy-start.19
  403.3 9.0 slice-start.3
  412.3 3.7 copy-start.44
  416.0 3.5 copy-start.43
  416.6 1.1 copy-start.9
  416.7 6.1 copy-start.35
  423.3 33.0 %copy-start.1 = (pred[256,2048]{1,0:T(8,128)(4,1)}, pred[256,2048]{1,0:T(8,128)(4,1)S(1)}, u32[]{:S(2)}) copy-start(pred[256,2048]{1,0:T(8,128)(4,1)S(1)} %broadcast_compare_fusion.5) | copy-start | bytes 1572868 | tf_op jit(solution)/shard_map/while
  473.2 4.6 copy-start
  493.1 10.8 slice-start
  497.9 6.0 slice-start.1
  497.9 6.0 copy-start.4
  513.7 33.0 %copy-start.1 = (pred[256,2048]{1,0:T(8,128)(4,1)}, pred[256,2048]{1,0:T(8,128)(4,1)S(1)}, u32[]{:S(2)}) copy-start(pred[256,2048]{1,0:T(8,128)(4,1)S(1)} %broadcast_compare_fusion.5) | copy-start | bytes 1572868 | tf_op jit(solution)/shard_map/while
  563.7 4.6 copy-start
  583.5 10.8 slice-start
  588.4 6.0 slice-start.1
  588.4 6.0 copy-start.4
  604.0 1.1 copy-start.13
  604.0 1.4 copy-start.15
  604.0 138.0 %reduce-scatter.11.cloned.1.call-start = ((), (), s32[]{:S(2)}) async-start(), calls=%async_computation.13 | async-start | bytes 7077888 | tf_op jit(solution)/shard_map/reduce_scatter | solution.py:219
  604.1 3.5 copy-start.8
  604.1 3.5 copy-start.24
  604.1 3.5 copy-start.30
  604.1 3.5 copy-start.34
  604.1 3.5 copy-start.38
  604.8 242.9 %reduce-scatter.13.cloned.1.call-start = ((), (), s32[]{:S(2)}) async-start(), calls=%async_computation.14 | async-start | bytes 2433024 | tf_op jit(solution)/shard_map/reduce_scatter | solution.py:237
  607.5 381.7 %reduce-scatter.15.cloned.1.call-start = ((), (), s32[]{:S(2)}) async-start(), calls=%async_computation.15 | async-start | bytes 9732096 | tf_op jit(solution)/shard_map/reduce_scatter | solution.py:241
  614.9 515.9 %reduce-scatter.17.cloned.1.call-start = ((), (), s32[]{:S(2)}) async-start(), calls=%async_computation.16 | async-start | bytes 9732096 | tf_op jit(solution)/shard_map/reduce_scatter | solution.py:243
  624.2 631.1 %reduce-scatter.19.cloned.1.call-start = ((), (), s32[]{:S(2)}) async-start(), calls=%async_computation.17 | async-start | bytes 7299072
  626.3 123.3 %copy-start.16 = (bf16[96,8,2,256]{3,1,2,0:T(8,128)(2,1)}, bf16[96,8,2,256]{3,1,2,0:T(8,128)(2,1)S(1)}, u32[]{:S(2)}) copy-start(bf16[96,8,2,256]{3,1,2,0:T(8,128)(2,1)S(1)} %copy.89) | copy-start | bytes 2359300
  672.9 76.8 %copy-start.17 = (bf16[512,768]{0,1:T(8,128)(2,1)}, bf16[512,768]{0,1:T(8,128)(2,1)S(1)}, u32[]{:S(2)}) copy-start(bf16[512,768]{0,1:T(8,128)(2,1)S(1)} %copy.62) | copy-start | bytes 2359300
  743.4 6.3 copy-start.18
  757.7 1.1 copy-start.3
  757.7 2.9 copy-start.26
  757.7 2.9 copy-start.27
  757.7 2.9 copy-start.28
  757.7 2.9 copy-start.32
  757.7 2.9 copy-start.41
  757.7 2.9 copy-start.42
  757.8 49.4 %copy-start.10 = (f32[512,768]{1,0:T(8,128)S(1)}, f32[512,768]{1,0:T(8,128)}, u32[]{:S(2)}) copy-start(f32[512,768]{1,0:T(8,128)} %copy-done.9) | copy-start | bytes 4718596
  757.8 49.4 %copy-start.36 = (f32[512]{0:T(512)S(1)}, f32[512]{0:T(512)}, u32[]{:S(2)}) copy-start(f32[512]{0:T(512)} %copy-done.35) | copy-start | bytes 6148
  (5 other events, 4.9 us)
Sparse Core Ops, SparseCore 0:
  11.0 59.7 all-gather.6
  78.5 62.3 all-gather.8
  143.1 63.3 all-gather.10
  209.3 54.0 all-gather.12
  266.2 61.9 all-gather.14
  331.1 61.9 all-gather.16
  604.1 67.2 reduce-scatter.8
  673.7 68.1 reduce-scatter.10
  747.9 99.7 reduce-scatter.12
  854.0 135.1 reduce-scatter.14
  995.7 135.0 reduce-scatter.16
  1136.9 118.4 reduce-scatter.18
where the time goes:
time: 1270 us; the launch traced here: 1260 us
  waiting for transfers between devices  747 us (59%)
  matrix products  246 us (19%)
  blocking collectives  93.6 us (7%)
  local copies, waits for them, and re-layouts  88.6 us (7%)
  other arithmetic  71.1 us (6%)
  between operations  15.1 us (1%)
    reduce_scatter x1, waiting for transfers between devices, on_device(): lax.psum_scatter(grad_w_back, ('dp', 'ctx'), scatter_dimension=0, tiled=T...  142 us
    reduce_scatter x1, waiting for transfers between devices, on_device(): lax.psum_scatter(grad_w_in, ('dp', 'ctx'), scatter_dimension=0, tiled=True)  142 us
    unnamed x13, waiting for transfers between devices  128 us
    unnamed x2, blocking collectives  81.7 us
    reduce_scatter x1, waiting for transfers between devices, on_device(): lax.psum_scatter(d_value_part.astype(jnp.bfloat16), 'ctx', scatter_dimens...  69.1 us
    all_gather x1, waiting for transfers between devices, on_device(): lax.all_gather(key_local, 'ctx', axis=1, tiled=True)  56.9 us
    reduce_scatter x1, waiting for transfers between devices, on_device(): lax.psum_scatter(d_key_part.astype(jnp.bfloat16), 'ctx', scatter_dimensio...  45.1 us
    all_gather x1, waiting for transfers between devices, on_device(): lax.all_gather(w_back, ('dp', 'ctx'), axis=0, tiled=True)  45.1 us
  transfers between devices with their start and end apart: 12, of which 11 were waited for; matrix products, arithmetic and copies ran while one was open for 15% of the time, Pallas kernels for 0%

commit v1 on v0

--- a/solution.py
+++ b/solution.py
@@ -1,14 +1,712 @@
+import functools
 import jax
 import jax.numpy as jnp
 from jax import lax
+from jax.experimental import pallas as pl
+from jax.experimental.pallas import tpu as pltpu
 from jax.sharding import PartitionSpec as P
 
 HEADS = 12
 HEAD_DIM = 64
+layer_eps = 1e-12
+MESH_ID = pl.DeviceIdType.MESH
+BF = jnp.bfloat16
+F32 = jnp.float32
+VMEM_LIMIT = 64 * 1024 * 1024 - 65536
+SCORE_SCALE = 0.125 * 1.4426950408889634
+EXCLUDE = -1e30
+
+
+def place():
+    d = lax.axis_index("dp")
+    t = lax.axis_index("ctx")
+    z = t // 2
+    c = t % 2
+    dx = d + 1 - 2 * (d % 2)
+    dy = (d + 2) % 4
+    return d, t, z, c, dx, dy
+
+
+def remote(src, dst, ss, rs, dev):
+    return pltpu.make_async_remote_copy(
+        src_ref=src, dst_ref=dst, send_sem=ss, recv_sem=rs, device_id=dev, device_id_type=MESH_ID
+    )
+
+
+def greet(devices):
+    bar = pltpu.get_barrier_semaphore()
+    for dev in devices:
+        pl.semaphore_signal(bar, inc=1, device_id=dev, device_id_type=MESH_ID)
+    pl.semaphore_wait(bar, len(devices))
+
+
+N_ARR = 5
+FIRST_X = (0, 1, 2)
+FIRST_Y = (3, 4)
+
+
+def gather_kernel(x, wi, wo, sm, wb, wq, xs, gi, go, gs, gb, gq,
+                  loc, s_x, r_x, s_xf, s_xd, r_xd, s_z, r_z, s_px, r_px, s_py, r_py, s_f, r_f, s_c, r_c):
+    d, t, z, c, dx, dy = place()
+    h = z // 2
+    zp = z + 1 - 2 * (z % 2)
+    inner = (z + h) % 2 == 1
+    dxy = (dx + 2) % 4
+    me = lambda zz: (d, zz * 2 + c)
+    core = (d, z * 2 + 1 - c)
+    nx, ny = (dx, t), (dy, t)
+    others = [(z + k) % 4 for k in (1, 2, 3)]
+    greet([me(zz) for zz in others] + [core, nx, ny])
+    sends = []
+
+    def go_(cp):
+        cp.start()
+        sends.append(cp)
+
+    own = [wi, wo, sm, wb]
+    dst = [gi, go, gs, gb, gq]
+    half = 128
+    for k in range(2):
+        rows = pl.ds(k * half, half)
+        go_(remote(x.at[1 - h, rows], xs.at[t, rows], s_x.at[0, k], r_x.at[z, k], me(2 - h)))
+        go_(remote(x.at[h, rows], xs.at[t, rows], s_x.at[1, k], r_x.at[z, k], me(zp)))
+    locals_ = [pltpu.make_async_copy(x.at[h], xs.at[t], loc.at[0])]
+    for a in range(4):
+        locals_.append(pltpu.make_async_copy(own[a], dst[a].at[d, z, c], loc.at[1 + a]))
+    locals_.append(pltpu.make_async_copy(wq.at[z % 2], gq.at[d, z, c], loc.at[5]))
+    for cp in locals_:
+        cp.start()
+
+    def mine(a, zz):
+        return wq.at[zz % 2] if a == 4 else own[a]
+
+    for a in (4, 3, 0, 1, 2):
+        for k in (1, 2, 3):
+            zz = others[k - 1]
+            go_(remote(mine(a, zz), dst[a].at[d, z, c], s_z.at[a, k - 1], r_z.at[a, z], me(zz)))
+
+    def plane(zz, first):
+        for a in (4, 3, 0, 1, 2):
+            src = mine(a, z) if first else dst[a].at[d, zz, c]
+            go_(remote(src, dst[a].at[d, zz, c], s_px.at[a, zz], r_px.at[a, zz], nx))
+            go_(remote(src, dst[a].at[d, zz, c], s_py.at[a, zz], r_py.at[a, zz], ny))
+
+    def got(ref, ss, rs, dev):
+        remote(ref, ref, ss, rs, dev).wait_recv()
+
+    def forward(zz):
+        for a in FIRST_Y:
+            got(dst[a].at[dy, zz, c], s_py.at[a, zz], r_py.at[a, zz], ny)
+            go_(remote(dst[a].at[dy, zz, c], dst[a].at[dy, zz, c], s_f.at[a, zz], r_f.at[a, zz], nx))
+        for a in FIRST_X:
+            got(dst[a].at[dx, zz, c], s_px.at[a, zz], r_px.at[a, zz], nx)
+            go_(remote(dst[a].at[dx, zz, c], dst[a].at[dx, zz, c], s_f.at[a, zz], r_f.at[a, zz], ny))
+
+    def across(zz):
+        for a in FIRST_Y:
+            got(dst[a].at[dx, zz, c], s_px.at[a, zz], r_px.at[a, zz], nx)
+            got(dst[a].at[dxy, zz, c], s_f.at[a, zz], r_f.at[a, zz], nx)
+        for a in FIRST_X:
+            got(dst[a].at[dy, zz, c], s_py.at[a, zz], r_py.at[a, zz], ny)
+            got(dst[a].at[dxy, zz, c], s_f.at[a, zz], r_f.at[a, zz], ny)
+        for a in range(N_ARR):
+            go_(remote(dst[a].at[:, zz, c], dst[a].at[:, zz, c], s_c.at[a, zz], r_c.at[a, zz], core))
+
+    plane(z, True)
+    far = [(2 * (1 - h) + j) for j in (0, 1)]
+    for k in range(2):
+        rows = pl.ds(k * half, half)
+        for j in (0, 1):
+            got(xs.at[far[j] * 2 + c, rows], s_x.at[0, k], r_x.at[far[j], k], me(2 - h))
+
+            @pl.when(inner)
+            def _(j=j, k=k, rows=rows):
+                remote(xs.at[far[j] * 2 + c, rows], xs.at[far[j] * 2 + c, rows],
+                       s_xf.at[j, k], r_x.at[far[j], k], me(zp)).start()
+
+    for cp in locals_:
+        cp.wait()
+    order = [z] + others
+    forward(z)
+    for zz in others[:1]:
+        for a in (4, 3, 0, 1, 2):
+            got(dst[a].at[d, zz, c], s_z.at[a, 0], r_z.at[a, zz], me(zz))
+        plane(zz, False)
+    across(z)
+    forward(others[0])
+    for zz in others[1:]:
+        for a in (4, 3, 0, 1, 2):
+            got(dst[a].at[d, zz, c], s_z.at[a, 0], r_z.at[a, zz], me(zz))
+        plane(zz, False)
+    for k in range(2):
+        rows = pl.ds(k * half, half)
+        got(xs.at[zp * 2 + c, rows], s_x.at[1, k], r_x.at[zp, k], me(zp))
+    for zz in (z, zp, far[0], far[1]):
+        go_(remote(xs.at[zz * 2 + c], xs.at[zz * 2 + c], s_xd.at[zz], r_xd.at[zz], core))
+    across(others[0])
+    forward(others[1])
+    forward(others[2])
+    across(others[1])
+    across(others[2])
+    for zz in order:
+        got(xs.at[zz * 2 + 1 - c], s_xd.at[zz], r_xd.at[zz], core)
+        for a in range(N_ARR):
+            ref = dst[a].at[:, zz, 1 - c]
+            got(ref, s_c.at[a, zz], r_c.at[a, zz], core)
+    for cp in sends:
+        cp.wait_send()
+
+    @pl.when(inner)
+    def _():
+        for k in range(2):
+            rows = pl.ds(k * half, half)
+            for j in (0, 1):
+                remote(xs.at[far[j] * 2 + c, rows], xs.at[far[j] * 2 + c, rows],
+                       s_xf.at[j, k], r_x.at[far[j], k], me(zp)).wait_send()
+
+
+def any_spec():
+    return pl.BlockSpec(memory_space=pl.ANY)
+
+
+def vmem_spec():
+    return pl.BlockSpec(memory_space=pltpu.VMEM)
+
+
+def dma(*shape):
+    return pltpu.SemaphoreType.DMA(shape)
+
+
+def gather_all(x, wi, wo, sm, wb, wq):
+    grid_of = lambda a: jax.ShapeDtypeStruct((4, 4, 2) + a.shape, a.dtype)
+    return pl.pallas_call(
+        gather_kernel,
+        out_shape=[
+            jax.ShapeDtypeStruct((8,) + x.shape[1:], x.dtype),
+            grid_of(wi), grid_of(wo), grid_of(sm), grid_of(wb), grid_of(wq[0]),
+        ],
+        in_specs=[any_spec()] * 6,
+        out_specs=[any_spec()] * 6,
+        scratch_shapes=[
+            dma(6), dma(2, 2), dma(4, 2), dma(2, 2), dma(4), dma(4), dma(N_ARR, 3), dma(N_ARR, 4),
+            dma(N_ARR, 4), dma(N_ARR, 4), dma(N_ARR, 4), dma(N_ARR, 4), dma(N_ARR, 4), dma(N_ARR, 4),
+            dma(N_ARR, 4), dma(N_ARR, 4),
+        ],
+        compiler_params=pltpu.CompilerParams(collective_id=1, has_side_effects=True),
+        name="gather_all",
+    )(x, wi, wo, sm, wb, wq)
+
+
+def exchange_kernel(a, b, loc, ss, rs):
+    d, t, z, c, dx, dy = place()
+    others = [(t + k) % 8 for k in range(1, 8)]
+    greet([(d, o) for o in others])
+    lc = pltpu.make_async_copy(a.at[t], b.at[t], loc)
+    lc.start()
+    cps = []
+    for k in (4, 3, 5, 2, 6, 1, 7):
+        cp = remote(a.at[others[k - 1]], b.at[t], ss.at[k - 1], rs.at[k - 1], (d, others[k - 1]))
+        cp.start()
+        cps.append(cp)
+    for k in range(1, 8):
+        src = (t + 8 - k) % 8
+        remote(b.at[src], b.at[src], ss.at[k - 1], rs.at[k - 1], (d, src)).wait_recv()
+    for cp in cps:
+        cp.wait_send()
+    lc.wait()
+
+
+def exchange(a, cid):
+    return pl.pallas_call(
+        exchange_kernel,
+        out_shape=jax.ShapeDtypeStruct(a.shape, a.dtype),
+        in_specs=[any_spec()],
+        out_specs=any_spec(),
+        scratch_shapes=[pltpu.SemaphoreType.DMA, dma(7), dma(7)],
+        compiler_params=pltpu.CompilerParams(collective_id=cid, has_side_effects=True),
+        name="exchange",
+    )(a)
+
+
+QB = 256
+KB = 256
+NH = 3
+
+
+def marks_of(ids_row):
+    kinds = lax.broadcasted_iota(jnp.int32, (16, ids_row.shape[1]), 0).astype(F32)
+    return kinds == ids_row
+
+
+def fill_keys_queries(qkv, ids, ka, qa):
+    hit = marks_of(ids[...])
+    ones = jnp.where(hit, 1.0, 0.0)
+    away = jnp.where(hit, 0.0, EXCLUDE).astype(BF)
+    for g in range(NH):
+        rows = slice(g * 64, (g + 1) * 64)
+        ka[g] = jnp.concatenate([qkv[1, rows].astype(F32), ones], axis=0).T.astype(BF)
+        qa[g, :64] = qkv[0, rows]
+        qa[g, 64:] = away
+
+
+def attn_fwd_kernel(lo, hi, qkv, ids, att, o32, lse, ka, va, qa):
+    n = qkv.shape[2]
+    fill_keys_queries(qkv, ids, ka, qa)
+    for g in range(NH):
+        va[g, :64] = qkv[2, g * 64:(g + 1) * 64]
+        va[g, 64:] = jnp.ones((16, n), BF)
+
+    def queries(i, _):
+        cols = pl.ds(pl.multiple_of(i * QB, QB), QB)
+
+        def block(j, carry):
+            at = pl.ds(pl.multiple_of(j * KB, KB), KB)
+            out = []
+            s = [jnp.dot(ka[g, at, :], qa[g, :, cols], preferred_element_type=F32) for g in range(NH)]
+            for g in range(NH):
+                m, acc = carry[g]
+                m2 = jnp.maximum(m, jnp.max(s[g], axis=0, keepdims=True))
+                p = jnp.exp2((s[g] - m2) * SCORE_SCALE).astype(BF)
+                acc = acc * jnp.exp2((m - m2) * SCORE_SCALE) + jnp.dot(
+                    va[g, :, at], p, preferred_element_type=F32)
+                out.append((m2, acc))
+            return tuple(out)
+
+        first = tuple((jnp.full((1, QB), -3e38, F32), jnp.zeros((80, QB), F32)) for _ in range(NH))
+        res = lax.fori_loop(lo[i], hi[i], block, first)
+        for g in range(NH):
+            m, acc = res[g]
+            total = acc[64:65]
+            o = acc[:64] / total
+            o32[i, g * 64:(g + 1) * 64] = o
+            att[i, g * 64:(g + 1) * 64] = o.astype(BF)
+            lse[g, pl.ds(i, 1)] = m * SCORE_SCALE + jnp.log2(total)
+        return 0
+
+    lax.fori_loop(0, n // QB, queries, 0)
+
+
+def smem_spec():
+    return pl.BlockSpec(memory_space=pltpu.SMEM)
+
+
+def attn_fwd(lo, hi, qkv, ids):
+    n = qkv.shape[2]
+    nq = n // QB
+    return pl.pallas_call(
+        attn_fwd_kernel,
+        in_specs=[smem_spec(), smem_spec(), vmem_spec(), vmem_spec()],
+        out_specs=[vmem_spec()] * 3,
+        scratch_shapes=[pltpu.VMEM((NH, n, 80), BF), pltpu.VMEM((NH, 80, n), BF), pltpu.VMEM((NH, 80, n), BF)],
+        out_shape=[
+            jax.ShapeDtypeStruct((nq, 192, QB), BF),
+            jax.ShapeDtypeStruct((nq, 192, QB), F32),
+            jax.ShapeDtypeStruct((NH, nq, QB), F32),
+        ],
+        compiler_params=pltpu.CompilerParams(vmem_limit_bytes=VMEM_LIMIT),
+        name="attn_fwd",
+    )(lo, hi, qkv, ids)
+
+
+def attn_bwd_kernel(lo, hi, qkv, ids, da, o32, lse, out, ka, qa, vk, dkv):
+    n = qkv.shape[2]
+    fill_keys_queries(qkv, ids, ka, qa)
+    for g in range(NH):
+        vk[g] = qkv[2, g * 64:(g + 1) * 64].astype(F32).T.astype(BF)
+    dkv[...] = jnp.zeros_like(dkv)
+
+    def queries(i, _):
+        cols = pl.ds(pl.multiple_of(i * QB, QB), QB)
+        fixed = []
+        for g in range(NH):
+            rows = slice(g * 64, (g + 1) * 64)
+            do = da[i, rows]
+            inner = jnp.sum(do.astype(F32) * o32[i, rows], axis=0, keepdims=True)
+            zero = jnp.zeros((64, QB), F32)
+            ra = jnp.concatenate([do.astype(F32), zero], axis=0).T.astype(BF)
+            rb = jnp.concatenate([zero, qkv[0, rows, cols].astype(F32)], axis=0).T.astype(BF)
+            fixed.append((inner, lse[g, pl.ds(i, 1)], ra, rb))
+
+        def block(j, carry):
+            at = pl.ds(pl.multiple_of(j * KB, KB), KB)
+            out = []
+            s = [jnp.dot(ka[g, at, :], qa[g, :, cols], preferred_element_type=F32) for g in range(NH)]
+            dp = [jnp.dot(vk[g, at, :], da[i, g * 64:(g + 1) * 64], preferred_element_type=F32) for g in range(NH)]
+            for g in range(NH):
+                inner, lse_i, ra, rb = fixed[g]
+                p = jnp.exp2(s[g] * SCORE_SCALE - lse_i)
+                ds = (p * (dp[g] - inner)).astype(BF)
+                dkv[g, at, :] += jnp.dot(p.astype(BF), ra, preferred_element_type=F32) + jnp.dot(
+                    ds, rb, preferred_element_type=F32)
+                out.append(carry[g] + jnp.dot(qkv[1, g * 64:(g + 1) * 64, at], ds, preferred_element_type=F32))
+            return tuple(out)
+
+        dq = lax.fori_loop(lo[i], hi[i], block, tuple(jnp.zeros((64, QB), F32) for _ in range(NH)))
+        for g in range(NH):
+            out[0, g * 64:(g + 1) * 64, cols] = (dq[g] * 0.125).astype(BF)
+        return 0
+
+    lax.fori_loop(0, n // QB, queries, 0)
+    for g in range(NH):
+        rows = slice(g * 64, (g + 1) * 64)
+        dkv_t = dkv[g].T
+        out[1, rows] = (dkv_t[64:] * 0.125).astype(BF)
+        out[2, rows] = dkv_t[:64].astype(BF)
+
+
+def attn_bwd(lo, hi, qkv, ids, da, o32, lse):
+    n = qkv.shape[2]
+    return pl.pallas_call(
+        attn_bwd_kernel,
+        in_specs=[smem_spec(), smem_spec()] + [vmem_spec()] * 5,
+        out_specs=vmem_spec(),
+        scratch_shapes=[
+            pltpu.VMEM((NH, n, 80), BF), pltpu.VMEM((NH, 80, n), BF), pltpu.VMEM((NH, n, 64), BF),
+            pltpu.VMEM((NH, n, 128), F32),
+        ],
+        out_shape=jax.ShapeDtypeStruct((3, 192, n), BF),
+        compiler_params=pltpu.CompilerParams(vmem_limit_bytes=VMEM_LIMIT),
+        name="attn_bwd",
+    )(lo, hi, qkv, ids, da, o32, lse)
+
+
+def scatter_kernel(dxp, di, do_, ds_, db, dq, ox, oi, oo, os_, ob, oq, *rest):
+    k_arr = 4
+    rd = rest[0:4]
+    r1 = rest[4:8]
+    r2 = rest[8:12]
+    r3 = rest[12:16]
+    r4 = rest[16:20]
+    r5 = rest[20:24]
+    (xd, x3, x4, x5, q0, q1, q2, qr,
+     s_d, r_d, s_1, r_1, s_2, r_2, s_3, r_3, s_4, r_4, s_5, r_5,
+     s_q1, r_q1, s_q2, r_q2, s_qe, r_qe) = rest[24:]
+    d, t, z, c, dx, dy = place()
+    x, y = d % 2, d // 2
+    h = z // 2
+    zp = z + 1 - 2 * (z % 2)
+    inner = (z + h) % 2 == 1
+    me = lambda zz: (d, zz * 2 + c)
+    core = (d, z * 2 + 1 - c)
+    nx, ny = (dx, t), (dy, t)
+    line = [(t + k) % 8 for k in range(1, 8)]
+    greet([(d, o) for o in line] + [nx, ny])
+    part = [di, do_, ds_, db]
+    outs = [oi, oo, os_, ob]
+    by_x = [True, True, True, False]
+    far = [2 * (1 - h), 2 * (1 - h) + 1]
+    order = [far[0], far[1], zp, z]
+    sends = []
+
+    def go_(cp):
+        cp.start()
+        sends.append(cp)
+
+    def got(ref, ss, rs, dev):
+        remote(ref, ref, ss, rs, dev).wait_recv()
+
+    for n_, zz in enumerate(order):
+        go_(remote(dxp.at[zz * 2 + 1 - c], xd.at[zz], s_d.at[4, n_], r_d.at[4, n_], core))
+    for n_, zz in enumerate(order):
+        for a in range(k_arr):
+            for yy in range(2):
+                go_(remote(part[a].at[yy, :, zz, 1 - c], rd[a].at[yy, :, zz], s_d.at[5 + 2 * a + yy, n_],
+                           r_d.at[5 + 2 * a + yy, n_], core))
+    go_(remote(dq.at[:, 1 - x], q1, s_q1, r_q1, nx))
+
+    def add_rows(dst, src):
+        n0 = dst.shape[0]
+
+        def step(i, _):
+            dst[i] = dst[i] + src[i]
+            return 0
+
+        lax.fori_loop(0, n0, step, 0)
+
+    def add_tok(dst, src):
+        def step(i, _):
+            at = pl.ds(pl.multiple_of(i * 32, 32), 32)
+            dst[at, :] = dst[at, :] + src[at, :]
+            return 0
+
+        lax.fori_loop(0, dst.shape[0] // 32, step, 0)
+
+    for n_, zz in enumerate(order):
+        got(xd.at[zz], s_d.at[4, n_], r_d.at[4, n_], core)
+        add_tok(xd.at[zz], dxp.at[zz * 2 + c])
+        if n_ == 2:
+            go_(remote(xd.at[zz], x5, s_5.at[4], r_5.at[4], me(zz)))
+
+        if n_ < 2:
+            @pl.when(jnp.logical_not(inner))
+            def _(n_=n_, zz=zz):
+                remote(xd.at[zz], x3.at[n_], s_3.at[4, n_], r_3.at[4, n_], me(zp)).start()
+
+    for n_, zz in enumerate(order):
+        for a in range(k_arr):
+            for yy in range(2):
+                got(rd[a].at[yy, :, zz], s_d.at[5 + 2 * a + yy, n_], r_d.at[5 + 2 * a + yy, n_], core)
+                for xx in range(2):
+                    add_rows(rd[a].at[yy, xx, zz], part[a].at[yy, xx, zz, c])
+            if by_x[a]:
+                go_(remote(rd[a].at[:, 1 - x, zz], r1[a].at[n_], s_1.at[a, n_], r_1.at[a, n_], nx))
+            else:
+                go_(remote(rd[a].at[1 - y, :, zz], r1[a].at[n_], s_1.at[a, n_], r_1.at[a, n_], ny))
+        if n_ == 0:
+            got(q1, s_q1, r_q1, nx)
+            for yy in range(2):
+                for zc in range(8):
+                    q0[yy, zc // 2, zc % 2] = q1[yy, zc // 2, zc % 2] + dq[yy, x, zc // 2, zc % 2]
+            go_(remote(q0.at[1 - y], q2, s_q2, r_q2, ny))
+        if n_ == 1:
+            for j in range(2):
+                @pl.when(inner)
+                def _(j=j):
+                    got(x3.at[j], s_3.at[4, j], r_3.at[4, j], me(zp))
+                    add_tok(xd.at[far[j]], x3.at[j])
+                    remote(xd.at[far[j]], x4, s_4.at[4, j], r_4.at[4], me(far[j])).start()
+        if n_ == 2:
+            got(q2, s_q2, r_q2, ny)
+            for zc in range(8):
+                q0[y, zc // 2, zc % 2] = q0[y, zc // 2, zc % 2] + q2[zc // 2, zc % 2]
+            for k in range(1, 8):
+                to = line[k - 1]
+                go_(remote(q0.at[y, to // 2, to % 2], qr.at[t], s_qe.at[k - 1], r_qe.at[k - 1], (d, to)))
+
+    for n_, zz in enumerate(order):
+        for a in range(k_arr):
+            if by_x[a]:
+                got(r1[a].at[n_], s_1.at[a, n_], r_1.at[a, n_], nx)
+                for yy in range(2):
+                    add_rows(rd[a].at[yy, x, zz], r1[a].at[n_, yy])
+                go_(remote(rd[a].at[1 - y, x, zz], r2[a].at[n_], s_2.at[a, n_], r_2.at[a, n_], ny))
+            else:
+                got(r1[a].at[n_], s_1.at[a, n_], r_1.at[a, n_], ny)
+                for xx in range(2):
+                    add_rows(rd[a].at[y, xx, zz], r1[a].at[n_, xx])
+                go_(remote(rd[a].at[y, 1 - x, zz], r2[a].at[n_], s_2.at[a, n_], r_2.at[a, n_], nx))
+
+    for n_, zz in enumerate(order):
+        for a in range(k_arr):
+            got(r2[a].at[n_], s_2.at[a, n_], r_2.at[a, n_], ny if by_x[a] else nx)
+            add_rows(rd[a].at[y, x, zz], r2[a].at[n_])
+            mine_ = rd[a].at[y, x]
+            if n_ < 2:
+                @pl.when(jnp.logical_not(inner))
+                def _(a=a, n_=n_, zz=zz, mine_=mine_):
+                    remote(mine_.at[zz], r3[a].at[n_], s_3.at[a, n_], r_3.at[a, n_], me(zp)).start()
+            elif n_ == 2:
+                go_(remote(mine_.at[zz], r5[a], s_5.at[a], r_5.at[a], me(zz)))
+    for n_ in range(2):
+        for a in range(k_arr):
+            @pl.when(inner)
+            def _(a=a, n_=n_):
+                mine_ = rd[a].at[y, x, far[n_]]
+                got(r3[a].at[n_], s_3.at[a, n_], r_3.at[a, n_], me(zp))
+                add_rows(mine_, r3[a].at[n_])
+                remote(mine_, r4[a], s_4.at[a, n_], r_4.at[a], me(far[n_])).start()
+    src_in = 2 - h
+    got(x5, s_5.at[4], r_5.at[4], me(zp))
+    got(x4, s_4.at[4, 0], r_4.at[4], me(src_in))
+
+    def tok(i, _):
+        at = pl.ds(pl.multiple_of(i * 32, 32), 32)
+        ox[h, at, :] = xd[z, at, :] + x5[at, :]
+        ox[1 - h, at, :] = x4[at, :]
+        return 0
+
+    lax.fori_loop(0, 8, tok, 0)
+    for k in range(1, 8):
+        src = (t + 8 - k) % 8
+        got(qr.at[src], s_qe.at[k - 1], r_qe.at[k - 1], (d, src))
+    qr[t] = q0[y, z, c]
+    for g in range(4):
+        oq[g] = qr[g].astype(F32) + qr[4 + g].astype(F32)
+    for a in range(k_arr):
+        got(r5[a], s_5.at[a], r_5.at[a], me(zp))
+        got(r4[a], s_4.at[a, 0], r_4.at[a], me(src_in))
+        acc = rd[a].at[y, x, z]
+        for i in range(acc.shape[0]):
+            outs[a][i] = acc[i].astype(F32) + r5[a][i].astype(F32) + r4[a][i].astype(F32)
+    for cp in sends:
+        cp.wait_send()
+    for n_ in range(2):
+        zz = far[n_]
+
+        @pl.when(jnp.logical_not(inner))
+        def _(n_=n_, zz=zz):
+            remote(xd.at[zz], x3.at[n_], s_3.at[4, n_], r_3.at[4, n_], me(zp)).wait_send()
+            for a in range(k_arr):
+                remote(rd[a].at[y, x, zz], r3[a].at[n_], s_3.at[a, n_], r_3.at[a, n_], me(zp)).wait_send()
+
+        @pl.when(inner)
+        def _(n_=n_, zz=zz):
+            remote(xd.at[zz], x4, s_4.at[4, n_], r_4.at[4], me(zz)).wait_send()
+            for a in range(k_arr):
+                remote(rd[a].at[y, x, zz], r4[a], s_4.at[a, n_], r_4.at[a], me(zz)).wait_send()
+
+
+def scatter_all(dxp, di, do_, ds_, db, dq):
+    arrs = [di, do_, ds_, db]
+    tails = [a.shape[4:] for a in arrs]
+    scratch = []
+    for lead in ((2, 2, 4), (4, 2), (4,), (2,), (), ()):
+        for a, tail in zip(arrs, tails):
+            scratch.append(pltpu.VMEM(lead + tail, a.dtype))
+    tok = dxp.shape[1:]
+    qt = dq.shape[4:]
+    scratch += [
+        pltpu.VMEM((4,) + tok, BF), pltpu.VMEM((2,) + tok, BF), pltpu.VMEM(tok, BF), pltpu.VMEM(tok, BF),
+        pltpu.VMEM((2, 4, 2) + qt, BF), pltpu.VMEM((2, 4, 2) + qt, BF), pltpu.VMEM((4, 2) + qt, BF),
+        pltpu.VMEM((8,) + qt, BF),
+        dma(13, 4), dma(13, 4), dma(4, 4), dma(4, 4), dma(4, 4), dma(4, 4), dma(5, 2), dma(5, 2),
+        dma(5, 2), dma(5), dma(5), dma(5),
+        pltpu.SemaphoreType.DMA, pltpu.SemaphoreType.DMA, pltpu.SemaphoreType.DMA, pltpu.SemaphoreType.DMA,
+        dma(7), dma(7),
+    ]
+    return pl.pallas_call(
+        scatter_kernel,
+        out_shape=[jax.ShapeDtypeStruct((2,) + tok, BF)]
+        + [jax.ShapeDtypeStruct(tail, F32) for tail in tails]
+        + [jax.ShapeDtypeStruct((4,) + qt, F32)],
+        in_specs=[vmem_spec()] * 6,
+        out_specs=[vmem_spec()] * 6,
+        scratch_shapes=scratch,
+        compiler_params=pltpu.CompilerParams(
+            collective_id=4, has_side_effects=True, vmem_limit_bytes=VMEM_LIMIT),
+        name="scatter_all",
+    )(dxp, di, do_, ds_, db, dq)
+
+
+def erf_parts(u):
+    phi_c = 0.5 * (1.0 + lax.erf(u * 0.7071067811865476))
+    return phi_c, phi_c + u * jnp.exp(-0.5 * u * u) * 0.3989422804014327
+
+
+def norm_forward(r):
+    center = r - jnp.mean(r, axis=-1, keepdims=True)
+    inv = lax.rsqrt(jnp.mean(center * center, axis=-1, keepdims=True) + layer_eps)
+    return center * inv, inv
+
+
+def norm_backward(n, inv, gain, dy):
+    gd = gain * dy
+    return (gd - jnp.mean(gd, axis=-1, keepdims=True) - n * jnp.mean(gd * n, axis=-1, keepdims=True)) * inv
+
+
+def on_device_fast(
+    inputs, segments, w_qkv, b_query, b_value, w_out, b_attn, gain_one, shift_one,
+    w_in, b_in, w_back, b_back, gain_two, shift_two, cotangent,
+):
+    nseq, span, width = inputs.shape
+    tokens = nseq * span
+    ff = w_in.shape[1]
+    depth = w_in.shape[0]
+    d, t, z, c, _, _ = place()
+    h = z // 2
+    group = (z % 2) * 2 + c
+    per = width // 4
+    vecs = (b_query, b_value, b_attn, gain_one, shift_one, b_back, gain_two, shift_two)
+    ffd = b_in.shape[0]
+    small = jnp.concatenate(
+        [v.astype(F32) for v in vecs] + [b_in.astype(F32), segments.astype(F32).reshape(-1)])
+    small = jnp.pad(small, (0, 1024 - small.shape[0])).reshape(8, 128)
+    wq = w_qkv.reshape(depth, 3, 2, 2 * per).transpose(2, 0, 1, 3).reshape(2, depth // 8, 8, 6 * per)
+    xs, gi, go, gs, gb, gq = gather_all(
+        inputs, w_in.reshape(depth // 8, 8, ff), w_out.reshape(depth // 8, 8, width), small,
+        w_back.reshape(ffd // 8, 8, width), wq)
+    wide_in = gi.reshape(width, ff)
+    wide_out = go.reshape(width, width)
+    wide_back = gb.reshape(ff, width)
+    flat = gs.reshape(32, 1024)
+    nv = len(vecs)
+    fv = flat[:, :nv * depth].reshape(32, nv, depth).transpose(1, 0, 2).reshape(nv, width)
+    full_b_in = flat[:, nv * depth:nv * depth + ffd].reshape(ff)
+    at = nv * depth + ffd
+    ids = lax.dynamic_index_in_dim(gs, d, 0, keepdims=False).reshape(8, 1024)[:, at:at + nseq * span]
+    ids = lax.dynamic_index_in_dim(ids.reshape(8, nseq, span), h, 1, keepdims=False)
+    n = 8 * span
+    ids_row = ids.reshape(1, n)
+    blocks = ids_row.reshape(n // QB, QB)
+    lo = (jnp.sum(ids_row < blocks[:, :1], axis=1) // KB).astype(jnp.int32)
+    hi = ((jnp.sum(ids_row <= blocks[:, -1:], axis=1) + KB - 1) // KB).astype(jnp.int32)
+    w_own = lax.dynamic_index_in_dim(gq.reshape(width, 3, 2, per), c, 2, keepdims=False).reshape(width, 3 * per)
+    bias_q = lax.dynamic_slice_in_dim(fv[0], group * per, per)
+    bias_v = lax.dynamic_slice_in_dim(fv[1], group * per, per)
+    bias = jnp.concatenate([bias_q, jnp.zeros_like(bias_q), bias_v])
+    xseq = xs.reshape(n, width)
+    qkv = jnp.einsum("kf,tk->ft", w_own, xseq, preferred_element_type=F32) + bias[:, None]
+    qkv = qkv.astype(BF).reshape(3, per, n)
+    att, o32, lse = attn_fwd(lo, hi, qkv, ids_row)
+    att = exchange(att, 2).reshape(nseq, width, span)
+
+    x32 = inputs.reshape(tokens, width).astype(F32)
+    attn_out = jnp.einsum("sit,id->std", att, wide_out, preferred_element_type=F32).reshape(tokens, width)
+    resid_one = x32 + attn_out + fv[2]
+    n1, inv1 = norm_forward(resid_one)
+    normed = n1 * fv[3] + fv[4]
+    normed_low = normed.astype(BF)
+    pre_act = jnp.dot(normed_low, wide_in, preferred_element_type=F32) + full_b_in
+    phi_c, slope = erf_parts(pre_act)
+    activ = (pre_act * phi_c).astype(BF)
+    branch = jnp.dot(activ, wide_back, preferred_element_type=F32) + fv[5]
+    n2, inv2 = norm_forward(normed + branch)
+    output = (n2 * fv[6] + fv[7]).astype(BF).reshape(nseq, span, width)
+    dy = cotangent.reshape(tokens, width).astype(F32)
+    d_two = norm_backward(n2, inv2, fv[6], dy)
+    d_branch = d_two.astype(BF)
+    grad_w_back = jnp.einsum("tf,td->fd", activ, d_branch, preferred_element_type=F32).astype(BF)
+    d_activ = jnp.einsum("td,fd->tf", d_branch, wide_back, preferred_element_type=F32)
+    d_pre = (d_activ * slope).astype(BF)
+    grad_w_in = jnp.einsum("td,tf->df", normed_low, d_pre, preferred_element_type=F32).astype(BF)
+    d_normed = d_two + jnp.einsum("tf,df->td", d_pre, wide_in, preferred_element_type=F32)
+    d_one = norm_backward(n1, inv1, fv[3], d_normed)
+    d_attn = d_one.astype(BF)
+    d_attn3 = d_attn.reshape(nseq, span, width)
+    grad_w_out = jnp.einsum("sit,std->id", att, d_attn3, preferred_element_type=F32).astype(BF)
+    d_att = jnp.einsum("std,id->sit", d_attn3, wide_out, preferred_element_type=F32).astype(BF)
+    d_att = exchange(d_att.reshape(8, per, span), 3)
+    d_proj = attn_bwd(lo, hi, qkv, ids_row, d_att, o32, lse)
+    proj = d_proj.reshape(3 * per, n)
+    dx_part = jnp.einsum("ft,kf->tk", proj, w_own, preferred_element_type=F32).astype(BF)
+    grad_w_qkv = jnp.einsum("tk,ft->kf", xseq, proj, preferred_element_type=F32).astype(BF)
+    g_bias = jnp.sum(d_proj.astype(F32), axis=2)
+    spread = jnp.zeros((2, width), F32)
+    spread = lax.dynamic_update_slice(spread, g_bias[::2], (0, group * per))
+    sums = [
+        spread[0], spread[1],
+        jnp.sum(d_attn.astype(F32), axis=0),
+        jnp.sum(d_normed * n1, axis=0),
+        jnp.sum(d_normed, axis=0),
+        jnp.sum(d_branch.astype(F32), axis=0),
+        jnp.sum(dy * n2, axis=0),
+        jnp.sum(dy, axis=0),
+    ]
+    g_in = jnp.sum(d_pre.astype(F32), axis=0)
+    g_small = jnp.concatenate(
+        [jnp.stack(sums).reshape(nv, 32, depth).transpose(1, 0, 2).reshape(32, nv * depth), g_in.reshape(32, ffd)],
+        axis=1)
+    g_small = jnp.pad(g_small, ((0, 0), (0, 1024 - g_small.shape[1])))
+    owner = (2, 2, 4, 2)
+    ox, oi, oo, os_, ob, oq = scatter_all(
+        dx_part.reshape(8, span, width),
+        grad_w_in.reshape(owner + (depth // 8, 8, ff)),
+        grad_w_out.reshape(owner + (depth // 8, 8, width)),
+        g_small.reshape(owner + (8, 128)),
+        grad_w_back.reshape(owner + (ffd // 8, 8, width)),
+        grad_w_qkv.reshape(owner + (depth // 8, 8, 3 * per)),
+    )
+    input_grad = d_one.reshape(nseq, span, width) + ox.astype(F32)
+    g_qkv = oq.reshape(4, depth, 3, per).transpose(1, 2, 0, 3).reshape(depth, 3 * width)
+    sv = os_.reshape(1024)
+    vec = lambda k: sv[k * depth:(k + 1) * depth]
+    return (
+        output, input_grad, g_qkv, vec(0), vec(1), oo.reshape(depth, width), vec(2), vec(3), vec(4),
+        oi.reshape(depth, ff), sv[nv * depth:nv * depth + ffd], ob.reshape(ffd, width), vec(5), vec(6), vec(7),
+    )
 
 
 negative_fill = -1e30
-layer_eps = 1e-12
 
 
 def layer_norm(resid, gain, shift):
@@ -74,7 +772,7 @@
     )
 
 
-def on_device(
+def on_device_general(
     inputs,
     segments,
     w_qkv,
@@ -283,8 +981,9 @@
         P(("dp", "ctx")),
         P("dp", "ctx", None),
     )
+    fits = mesh.shape["dp"] == 4 and mesh.shape["ctx"] == 8
     return jax.shard_map(
-        on_device,
+        on_device_fast if fits else on_device_general,
         mesh=mesh,
         in_specs=placed,
         out_specs=(

time: 1270 us -> 396 us (0.31)
  waiting for transfers between devices: 747 us -> 0 us
  Pallas kernels: 0 us -> 276 us
  matrix products: 246 us -> 61.6 us
  blocking collectives: 93.6 us -> 0 us
  other arithmetic: 71.1 us -> 12.2 us
  local copies, waits for them, and re-layouts: 88.6 us -> 40.1 us
  between operations: 15.1 us -> 1.69 us
    reduce_scatter x5 -> x0, waiting for transfers between devices: 432 us -> none  [the longest x1 142 us: on_device(): lax.psum_scatter(grad_w_back, ('dp', 'ctx'), scatter_dimension=0, tiled=T...]
    pallas_call x0 -> x6, Pallas kernels: none -> 276 us  [the longest x1 98.8 us: gather_all(): pl.pallas_call(gather_kernel, out_shape=[jax.ShapeDtypeStruct((8,) + x.sh...]
    all_gather x6 -> x0, waiting for transfers between devices: 187 us -> none  [the longest x1 56.9 us: on_device(): lax.all_gather(key_local, 'ctx', axis=1, tiled=True)]
    dot_general x26 -> x12, matrix products: 246 us -> 61.6 us  [the longest x1 8.48 us: on_device_fast(): jnp.dot(normed_low, wide_in, preferred_element_type=F32) + full_b_in]
    unnamed x13 -> x0, waiting for transfers between devices: 128 us -> none
    unnamed x2 -> x0, blocking collectives: 81.7 us -> none
    convert_element_type x12 -> x0, other arithmetic: 39 us -> none  [the longest x2 33.7 us: attend_backward(): d_scores = (probs * (d_probs - inner)).astype(jnp.bfloat16)]
    dynamic_update_slice x6 -> x1, local copies, waits for them, and re-layouts: 27.2 us -> 0.15 us  [on_device_fast(): spread = lax.dynamic_update_slice(spread, g_bias[::2], (0, group * per))]
  transfers between devices with their start and end apart: 12 -> 0, of which waited for: 11 -> 0; matrix products, arithmetic and copies ran while one was open for 15% -> 0% of each run, Pallas kernels for 0% -> 0%
where the time goes in v1:
time: 396 us; the launch traced here: 391 us
  Pallas kernels  276 us (70%)
  matrix products  61.6 us (16%)
  local copies, waits for them, and re-layouts  40.1 us (10%)
  other arithmetic  12.2 us (3%)
    pallas_call x1, Pallas kernels, gather_all(): pl.pallas_call(gather_kernel, out_shape=[jax.ShapeDtypeStruct((8,) + x.sh...  98.8 us
    pallas_call x1, Pallas kernels, scatter_all(): pl.pallas_call(scatter_kernel, out_shape=[jax.ShapeDtypeStruct((2,) + tok...  87.7 us
    pallas_call x2, Pallas kernels, exchange(): pl.pallas_call(exchange_kernel, out_shape=jax.ShapeDtypeStruct(a.shape, a...  39.1 us
    pallas_call x1, Pallas kernels, attn_bwd(): pl.pallas_call(attn_bwd_kernel, in_specs=[smem_spec(), smem_spec()] + [vm...  28.5 us
    pallas_call x1, Pallas kernels, attn_fwd(): pl.pallas_call(attn_fwd_kernel, in_specs=[smem_spec(), smem_spec(), vmem_...  21.8 us
    dynamic_slice x2, local copies, waits for them, and re-layouts, on_device_fast(): lax.dynamic_index_in_dim(gq.reshape(width, 3, 2, per), c, 2, keepdims=False)  9.27 us
    dot_general x1, matrix products, on_device_fast(): jnp.dot(normed_low, wide_in, preferred_element_type=F32) + full_b_in  8.48 us
    dot_general x1, matrix products, on_device_fast(): jnp.einsum('td,fd->tf', d_branch, wide_back, preferred_element_type=F32)  8.37 us

profile of v1, /device:TPU:28, one launch (start us, length us, event | category | flops | bytes accessed | tf_op | source)
XLA Modules:
  0.0 391.5 jit_solution(11357772212585390908)
XLA Ops:
  0.7 0.9 reshape.248
  1.7 0.7 reshape.249.wq
  2.4 0.7 convert_bitcast_fusion
  3.1 6.1 %concatenate.10 = f32[800]{0:T(1024)S(1)} concatenate(bf16[24]{0:T(256)(128)(2,1)} %param.19, bf16[24]{0:T(256)(128)(2,1)} %param.20, bf16[24]{0:T(256)(128)(2,1)} %param.22, bf16[24]{0:T(256)(128)(2,1)} %param.23, bf16[24]{0:T(256)(128)(2,1)} %param.24, bf16[24]{0:T(256)(128)(2,1)} %param.28, bf16[24]{0:T(256)(128)(2,1)} %param.29, bf16[24]{0:T(256)(128)(2,1)} %param.30, ...), dimensions={0} | concatenate | bytes 5824 | tf_op jit(solution)/shard_map/concatenate | solution.py:611
  9.2 0.6 pad_bitcast_fusion.sm
  9.8 98.8 %gather_all.1 = (bf16[8,256,768]{2,1,0:T(8,128)(2,1)}, bf16[4,4,2,3,8,3072]{5,4,3,2,1,0:T(8,128)(2,1)}, bf16[4,4,2,3,8,768]{5,4,3,2,1,0:T(8,128)(2,1)}, f32[4,4,...) custom-call(bf16[2,256,768]{2,1,0:T(8,128)(2,1)} %x.5, ...), custom_call_target="tpu_custom_call" | custom-call | tf_op jit(solution)/shard_map/gather_all/pallas_call | solution.py:182
  108.6 0.9 copy.66
  109.5 0.6 copy-done.13
  110.2 0.1 reshape.256
  110.3 0.9 slice_reduce_fusion.1
  111.6 6.3 %reshape.252 = bf16[768,3,2,192]{3,2,1,0:T(2,128)(2,1)S(1)} reshape(bf16[4,4,2,3,8,1152]{5,4,3,2,1,0:T(8,128)(2,1)} %get-tuple-element.31) | data formatting | bytes 3538944 | tf_op jit(solution)/shard_map/reshape | solution.py:633
  117.9 3.8 constant_dynamic-slice_fusion
  121.7 5.4 %copy.50 = bf16[768,3,1,192]{0,3,1,2:T(8,128)(2,1)S(1)} copy(bf16[768,3,1,192]{3,2,1,0:T(2,128)(2,1)} %constant_dynamic-slice_fusion) | data formatting | bytes 1769472 | tf_op jit(solution)/shard_map/jit(dynamic_index_in_dim)/dynamic_slice | solution.py:633
  127.2 5.7 %add_convert_fusion = bf16[576,2048]{1,0:T(8,128)(2,1)} fusion(bf16[768,576]{0,1:T(8,128)(2,1)S(1)} %bitcast.130, bf16[2048,768]{1,0:T(8,128)(2,1)} %bitcast.170, f32[576]{0:T(1024)S(1)} %pad_maximum_fusion), kind=kOutput, calls=%fused_computation.13 | convolution fusion | flops 1814298624 | bytes 6392064 | tf_op jit(solution)/shard_map/kf,tk->ft/dot_general | solution.py:638
  132.9 0.8 constant_dynamic-slice_fusion.2
  133.7 0.6 copy.59
  134.3 0.1 copy.49
  134.5 0.2 convert_reduce_fusion.5
  134.7 0.5 and_select_fusion
  135.3 21.8 %attn_fwd.1 = (bf16[8,192,256]{2,1,0:T(8,128)(2,1)}, f32[8,192,256]{2,1,0:T(8,128)}, f32[3,8,256]{2,1,0:T(8,128)}) custom-call(s32[8]{0:T(128)} %get-tuple-element.89.lo, s32[8]{0:T(128)} %get-tuple-element.88.hi, bf16[3,192,2048]{2,1,0:T(8,128)(2,1)} %bitcast.117, f32[1,2048]{1,0:T(1,128)} %bitcast.156), custom_call_target="tpu_custom_call" | custom-call | tf_op jit(solution)/shard_map/attn_fwd/pallas_call | solution.py:296
  157.1 18.6 %exchange.2 = bf16[8,192,256]{2,1,0:T(8,128)(2,1)} custom-call(bf16[8,192,256]{2,1,0:T(8,128)(2,1)} %get-tuple-element.33.a), custom_call_target="tpu_custom_call" | custom-call | tf_op jit(solution)/shard_map/exchange/pallas_call | solution.py:220
  175.7 1.4 copy.51
  177.1 0.1 add.144
  177.2 2.1 fusion.23
  179.4 0.3 multiply_reduce_fusion.3
  179.7 0.4 copy-done.20
  180.3 0.8 slice.114
  181.2 8.5 %multiply_convert_fusion = (bf16[512,3072]{1,0:T(8,128)(2,1)}, f32[512,3072]{1,0:T(8,128)}) fusion(f32[3072]{0:T(1024)S(1)} %add.151, bf16[768,3072]{1,0:T(8,128)(2,1)} %bitcast.164, f32[512,768]{1,0:T(8,128)S(1)} %get-tuple-element.80, f32[768]{0:T(1024)S(1)} %add.148, f32[768]{0:T(1024)S(1)} %mul.148, f32[512]{0:T(512)S(1)} %add_rsqrt_fusion.1, ...), kind=kOutput, calls=%fused_computation.8 | convolution fusion | flops 2427322368 | bytes 15751168 | tf_op jit(solution)/shard_map/dot_general | solution.py:649
  189.7 0.1 add.156
  189.8 6.0 %fusion.24 = (f32[512]{0:T(512)S(1)}, f32[512,768]{1,0:T(8,128)S(1)}) fusion(f32[768]{0:T(1024)S(1)} %add.156, bf16[512,3072]{1,0:T(8,128)(2,1)} %get-tuple-element.81, bf16[3072,768]{1,0:T(8,128)(2,1)} %bitcast.168, f32[768]{0:T(1024)S(1)} %add.148, f32[768]{0:T(1024)S(1)} %mul.148, f32[512]{0:T(512)S(1)} %add_rsqrt_fusion.1, ...), kind=kOutput, calls=%fused_computation.99 | convolution fusion | flops 2418671104 | bytes 11025408 | tf_op jit(solution)/shard_map/dot_general | solution.py:652
  195.9 0.3 multiply_reduce_fusion.2
  196.2 0.4 copy-done.17
  196.7 0.3 copy-done.1
  197.0 1.2 fusion.13
  198.2 0.9 convert_reduce_fusion.2
  199.2 2.3 convert_reduce_fusion.3
  201.5 8.4 %convert_reduce_fusion = (f32[3072]{0:T(1024)}, bf16[512,3072]{1,0:T(8,128)(2,1)S(1)}) fusion(f32[512,3072]{1,0:T(8,128)} %get-tuple-element.82, f32[3072]{0:T(1024)S(1)} %add.151, bf16[3072,768]{1,0:T(8,128)(2,1)} %bitcast.169, f32[512,768]{1,0:T(8,128)S(1)} %get-tuple-element.64), kind=kOutput, calls=%fused_computation.7 | convolution fusion | flops 2436756480 | bytes 15753216 | tf_op jit(solution)/shard_map/td,fd->tf/dot_general | solution.py:659
  209.9 3.6 multiply_reduce_fusion
  213.6 2.3 convert_reduce_fusion.4
  215.9 1.7 convolution_convert_fusion.4
  217.6 20.5 %exchange.3.da = bf16[8,192,256]{2,1,0:T(8,128)(2,1)} custom-call(bf16[8,192,256]{2,1,0:T(8,128)(2,1)} %bitcast.134), custom_call_target="tpu_custom_call" | custom-call | tf_op jit(solution)/shard_map/exchange/pallas_call | solution.py:220
  238.1 28.5 %attn_bwd.1 = bf16[3,192,2048]{2,1,0:T(8,128)(2,1)} custom-call(s32[8]{0:T(128)} %get-tuple-element.89.lo, s32[8]{0:T(128)} %get-tuple-element.88.hi, bf16[3,192,2048]{2,1,0:T(8,128)(2,1)} %bitcast.118, f32[1,2048]{1,0:T(1,128)} %bitcast.157, bf16[8,192,256]{2,1,0:T(8,128)(2,1)} %exchange.3.da, f32[8,192,256]{2,1,0:T(8,128)} %get-tuple-element.37.o32, ...), custom_call_target="tpu_custom_call" | custom-call | tf_op jit(solution)/shard_map/attn_bwd/pallas_call | solution.py:359
  266.6 4.6 %convolution_convert_fusion.3 = bf16[768,576]{0,1:T(8,128)(2,1)S(1)} fusion(bf16[576,2048]{1,0:T(8,128)(2,1)} %bitcast.119, bf16[2048,768]{1,0:T(8,128)(2,1)} %bitcast.171), kind=kOutput, calls=%fused_computation.42 | convolution fusion | flops 1812381696 | bytes 6389760 | tf_op jit(solution)/shard_map/tk,ft->kf/dot_general | solution.py:672
  271.2 1.3 copy.53
  272.5 7.3 %convolution_convert_fusion = bf16[3072,768]{1,0:T(8,128)(2,1)} fusion(bf16[512,3072]{1,0:T(8,128)(2,1)} %get-tuple-element.81, f32[512,768]{1,0:T(8,128)} %copy-done.6), kind=kOutput, calls=%fused_computation.10 | convolution fusion | flops 2418671616 | bytes 9437184 | tf_op jit(solution)/shard_map/tf,td->fd/dot_general | solution.py:658
  279.9 0.4 convert_reduce_fusion.1
  280.3 0.2 dynamic_update_slice.3
  280.5 0.1 stack.24
  281.2 0.1 copy.52
  281.3 0.1 reshape.271
  281.6 0.7 copy.61
  282.3 3.0 bitcast_convert_fusion
  285.4 6.6 %convolution_convert_fusion.1 = bf16[768,3072]{1,0:T(8,128)(2,1)} fusion(bf16[512,3072]{1,0:T(8,128)(2,1)} %copy-done.39, f32[512,768]{1,0:T(8,128)S(1)} %copy-done.4, f32[768]{0:T(1024)S(1)} %copy-done.34, f32[768]{0:T(1024)S(1)} %copy-done.27, f32[512]{0:T(512)S(1)} %copy-done.32, f32[512]{0:T(512)S(1)} %copy-done.23), kind=kOutput, calls=%fused_computation.11 | convolution fusion | flops 2420244480 | bytes 9447424 | tf_op jit(solution)/shard_map/td,tf->df/dot_general | solution.py:661
  292.0 4.0 %convolution_convert_fusion.2 = bf16[2048,768]{1,0:T(8,128)(2,1)} fusion(bf16[576,2048]{1,0:T(8,128)(2,1)S(1)} %bitcast.120, bf16[768,576]{0,1:T(8,128)(2,1)S(1)} %bitcast.131), kind=kOutput, calls=%fused_computation.14 | convolution fusion | flops 1813512192 | bytes 6389760 | tf_op jit(solution)/shard_map/ft,kf->tk/dot_general | solution.py:671
  296.0 87.7 %scatter_all.1 = (bf16[2,256,768]{2,1,0:T(8,128)(2,1)}, f32[3,8,3072]{2,1,0:T(8,128)}, f32[3,8,768]{2,1,0:T(8,128)}, f32[8,128]{1,0:T(8,128)}, f32[12,8,768]{2,1,0:T(8,128)}, /*index=5*/f32[4,3,8,576]{3,2,1,0:T(8,128)}) custom-call(bf16[8,256,768]{2,1,0:T(8,128)(2,1)} %bitcast.125, bf16[2,2,4,2,3,8,3072]{6,5,4,3,2,1,0:T(8,128)(2,1)} %bitcast.123, ...), custom_call_target="tpu_custom_call" | custom-call | tf_op jit(solution)/shard_map/scatter_all/pallas_call | solution.py:567
  383.7 2.9 convert_add_fusion.1
  386.7 0.2 reshape.276
  386.9 0.2 copy.54
  387.1 0.9 reshape.277
  388.0 0.6 fusion.22
  388.6 0.6 slice.101
  389.2 0.6 copy.78
  389.8 0.7 copy.79
  390.5 0.7 copy.80
  (128 shorter events, 1.9 us)
Async XLA Ops:
  109.5 0.7 copy-start.13
  127.2 5.7 %copy-start.7 = (bf16[768,3,1,192]{0,3,1,2:T(8,128)(2,1)}, bf16[768,3,1,192]{0,3,1,2:T(8,128)(2,1)S(1)}, u32[]{:S(2)}) copy-start(bf16[768,3,1,192]{0,3,1,2:T(8,128)(2,1)S(1)} %copy.50) | copy-start | bytes 2654212
  157.1 20.1 %copy-start.21 = (f32[32,24]{1,0:T(8,128)S(1)}, f32[32,24]{1,0:T(8,128)}, u32[]{:S(2)}) copy-start(f32[32,24]{1,0:T(8,128)} %get-tuple-element.58) | copy-start | bytes 9220
  157.1 20.1 %copy-start.9 = (bf16[2,256,768]{2,1,0:T(8,128)(2,1)S(1)}, bf16[2,256,768]{2,1,0:T(8,128)(2,1)}, u32[]{:S(2)}) copy-start(bf16[2,256,768]{2,1,0:T(8,128)(2,1)} %x.5) | copy-start | bytes 2359300
  179.4 10.4 %copy-start.2 = (f32[512,768]{1,0:T(8,128)}, f32[512,768]{1,0:T(8,128)S(1)}, u32[]{:S(2)}) copy-start(f32[512,768]{1,0:T(8,128)S(1)} %get-tuple-element.80) | copy-start | bytes 4718596
  179.4 0.7 copy-start.20
  179.4 0.8 copy-start.19
  179.4 34.1 %copy-start.22 = (f32[512]{0:T(512)}, f32[512]{0:T(512)S(1)}, u32[]{:S(2)}) copy-start(f32[512]{0:T(512)S(1)} %broadcast_multiply_fusion.4) | copy-start | bytes 6148
  179.7 33.8 %copy-start.31 = (f32[512]{0:T(512)}, f32[512]{0:T(512)S(1)}, u32[]{:S(2)}) copy-start(f32[512]{0:T(512)S(1)} %add_rsqrt_fusion.1) | copy-start | bytes 6148
  180.2 33.4 %copy-start.26 = (f32[768]{0:T(1024)}, f32[768]{0:T(1024)S(1)}, u32[]{:S(2)}) copy-start(f32[768]{0:T(1024)S(1)} %mul.148) | copy-start | bytes 9220
  180.3 9.5 %copy-start.33 = (f32[768]{0:T(1024)}, f32[768]{0:T(1024)S(1)}, u32[]{:S(2)}) copy-start(f32[768]{0:T(1024)S(1)} %add.148) | copy-start | bytes 9220
  181.2 8.5 %copy-start.18 = (f32[32,24]{1,0:T(8,128)S(1)}, f32[32,24]{1,0:T(8,128)}, u32[]{:S(2)}) copy-start(f32[32,24]{1,0:T(8,128)} %get-tuple-element.55) | copy-start | bytes 9220
  195.9 0.7 copy-start.17
  195.9 1.1 copy-start.1
  197.0 2.1 copy-start.16
  199.2 10.7 %slice-start = ((s8[4718592]{0:T(1024)(128)(4,1)}), s8[4194304]{0:T(1024)(128)(4,1)S(1)}, s32[]{:S(2)}) async-start(s8[4718592]{0:T(1024)(128)(4,1)} %bitcast.165), calls=%async_computation | async-start | bytes 8388608
  201.5 8.4 %copy-start.6 = (f32[512,768]{1,0:T(8,128)}, f32[512,768]{1,0:T(8,128)S(1)}, u32[]{:S(2)}) copy-start(f32[512,768]{1,0:T(8,128)S(1)} %get-tuple-element.64) | copy-start | bytes 4718596
  201.5 8.4 %copy-start.3 = (f32[512,768]{1,0:T(8,128)S(1)}, f32[512,768]{1,0:T(8,128)}, u32[]{:S(2)}) copy-start(f32[512,768]{1,0:T(8,128)} %copy-done.2) | copy-start | bytes 4718596
  201.5 8.4 %slice-start.1 = ((s8[4718592]{0:T(1024)(128)(4,1)}), s8[524288]{0:T(1024)(128)(4,1)S(1)}, s32[]{:S(2)}) async-start(s8[4718592]{0:T(1024)(128)(4,1)} %bitcast.165), calls=%async_computation.1 | async-start | bytes 1048576
  209.9 3.7 copy-start.39
  213.6 2.3 copy-start.38
  215.8 1.7 copy-start.10
  272.5 7.3 %copy-start = (bf16[3,192,2048]{2,1,0:T(8,128)(2,1)S(1)}, bf16[3,192,2048]{2,1,0:T(8,128)(2,1)}, u32[]{:S(2)}) copy-start(bf16[3,192,2048]{2,1,0:T(8,128)(2,1)} %attn_bwd.1) | copy-start | bytes 7077892
  279.8 0.8 copy-start.29
  279.8 0.9 copy-start.36
  279.8 1.0 copy-start.35
  279.8 1.1 copy-start.28
  279.8 1.2 copy-start.25
  279.8 1.3 copy-start.24
  279.9 1.6 copy-start.30
  279.9 2.4 copy-start.5
  282.3 3.1 copy-start.4
  282.3 3.1 copy-start.23
  282.3 3.1 copy-start.27
  282.3 3.1 copy-start.32
  282.3 3.1 copy-start.34
  285.4 6.6 %copy-start.8 = (bf16[768,3,1,192]{0,3,1,2:T(8,128)(2,1)S(1)}, bf16[768,3,1,192]{0,3,1,2:T(8,128)(2,1)}, u32[]{:S(2)}) copy-start(bf16[768,3,1,192]{0,3,1,2:T(8,128)(2,1)} %copy-done.7) | copy-start | bytes 2654212
  383.7 3.0 copy-start.14
  386.7 1.3 copy-start.37
  386.7 2.5 copy-start.15
  386.7 3.1 copy-start.12
  386.7 3.8 copy-start.11
